TPU v7x, 512 devices: a whole 4x8x8 slice. The times are simulated.
512 devices in a mesh: row: 16 (over y, core), col: 32 (over z, x).
Axes of the slice: x: 4, y: 8, z: 8, core: 2. Of those that a mesh axis runs over, the one named last changes fastest.
Arguments:
- src_embed: bfloat16 [64, 32768], P('col', 'row'), may hold values from -1.5 to 1.5
- src_left: bfloat16 [64, 32768], P('col', 'row'), may hold values from -0.75 to 0.75
- src_right: bfloat16 [64, 32768], P('col', 'row'), may hold values from -4.5 to 4.5, as said below
- src_logit: float32 [32768], P('row'), may hold values from -2 to 3.2
- src_weight: float32 [32768], P('row'), may hold values from 1 to 10
- tgt_embed: bfloat16 [64, 65536], P('row', 'col'), may hold values from -1.5 to 1.5
- tgt_left: bfloat16 [64, 65536], P('row', 'col'), may hold values from -0.75 to 0.75
- tgt_right: bfloat16 [64, 65536], P('row', 'col'), may hold values from -4.5 to 4.5, as said below
- tgt_logit: float32 [65536], P('col'), may hold values from -2 to 3.2
- tgt_weight: float32 [65536], P('col'), may hold values from 1 to 10
Outputs:
- row_potential: float32 [32768], P('row')
- col_potential: float32 [65536], P('col')
- new_core: float32 [64, 64], replicated
Inputs may be any that keep to these rules, and one draw needn't show every extreme that they name: `src_right`: each rank's row sums to about zero over the points. `tgt_right`: each rank's row sums to about zero over the points.
All inputs are finite; a program needn't handle non-finite values.
Results may differ from a plain program's by a relative error of at most 0.012.
Values may be sent and summed in bfloat16 or wider, within the bound.
No kernel may reach another device: no remote copies, remote signals or barrier semaphores. Data moves between devices by JAX's collectives and lax.ppermute only.
A program may use at most 64 MiB of HBM per device.

v0:
```python
import math

import jax
import jax.numpy as jnp
from jax import lax
from jax.sharding import Mesh
from jax.sharding import PartitionSpec as P

SWEEPS = 3
ROW = ("row_0", "row_1")
COL = ("col_0", "col_1")
ROW_COL = ("row_0", "row_1", "col_0", "col_1")


def in_one_piece(arrays, axis, dim, along):
    ends, at = ([], 0)
    for a in arrays[:-1]:
        at += a.shape[along]
        ends.append(at)
    both = jnp.concatenate(arrays, axis=along)
    return tuple(jnp.split(lax.all_gather(both, axis, axis=dim, tiled=True), ends, axis=along))


def over_axes(value, axes):
    for axis in axes:
        value = lax.psum(value, axis)
    return value


def sent_to_all(value, axis):
    peers = lax.axis_size(axis)
    return lax.all_to_all(
        jnp.broadcast_to(value[None], (peers, *value.shape)), axis, 0, 0, tiled=True
    )


def taken_together(value, axis):
    return sent_to_all(value, axis).sum(axis=0)


def inner_dot(left_side, right_side):
    return lax.dot_general(
        left_side, right_side, (((0,), (0,)), ((), ())), preferred_element_type=jnp.float32
    )


def body(
    src_embed,
    src_left,
    src_right,
    src_logit,
    src_weight,
    tgt_embed,
    tgt_left,
    tgt_right,
    tgt_logit,
    tgt_weight,
):
    highest = lax.Precision.HIGHEST
    row_count = src_logit.shape[0]
    col_count = tgt_logit.shape[0]
    n_all = row_count * lax.axis_size(ROW)
    m_all = col_count * lax.axis_size(COL)
    embed_full, left_full, right_full = in_one_piece((src_embed, src_left, src_right), COL, 0, 1)
    tgt_embed_full, tgt_left_full, tgt_right_full = in_one_piece(
        (tgt_embed, tgt_left, tgt_right), ROW, 0, 1
    )
    rank_width = tgt_embed_full.shape[0]
    embed_scaled = embed_full * 0.125
    block_rows = 512
    block_count = row_count // block_rows
    positions = jnp.arange(block_count, dtype=jnp.int32)

    def opening(position):
        start_row = position * block_rows
        embed_rows = lax.dynamic_slice_in_dim(embed_scaled, start_row, block_rows, 1)
        logit_rows = lax.dynamic_slice_in_dim(src_logit, start_row, block_rows, 0)
        start_tile = jnp.exp(
            logit_rows[:, None] + tgt_logit[None, :] + inner_dot(embed_rows, tgt_embed_full)
        ).astype(jnp.bfloat16)
        tile_total = jnp.sum(start_tile, dtype=jnp.float32)
        side_rows = lax.dot_general(
            start_tile, tgt_right_full, (((1,), (1,)), ((), ())), preferred_element_type=jnp.float32
        )
        return (tile_total, side_rows)

    tile_totals, side_rows = lax.map(opening, positions)
    side_sum = side_rows.reshape(row_count, rank_width)
    local_total = jnp.sum(tile_totals)
    core_part = jnp.dot(right_full.astype(jnp.float32), side_sum, precision=highest)
    src_part = jnp.sum(src_weight) / lax.axis_size(COL)
    tgt_part = jnp.sum(tgt_weight) / lax.axis_size(ROW)
    grand_total, core_sum, src_mass, tgt_mass = (
        over_axes(local_total, ROW_COL),
        over_axes(core_part, ROW_COL),
        over_axes(src_part, ROW_COL),
        over_axes(tgt_part, ROW_COL),
    )
    mass_scale = math.sqrt(n_all * m_all)
    mixing = mass_scale * core_sum / grand_total
    row_factor = (2.0 * jnp.dot(mixing.T, left_full.astype(jnp.float32), precision=highest)).astype(
        jnp.bfloat16
    )
    left_stack = jnp.concatenate([embed_scaled, row_factor], axis=0)
    right_stack = jnp.concatenate([tgt_embed_full, tgt_left_full], axis=0)
    log_shift = -jnp.log(grand_total)

    def kernel_rows(position):
        start_row = position * block_rows
        left_rows = lax.dynamic_slice_in_dim(left_stack, start_row, block_rows, 1)
        logit_rows = lax.dynamic_slice_in_dim(src_logit, start_row, block_rows, 0)
        return jnp.exp(
            logit_rows[:, None] + tgt_logit[None, :] + log_shift + inner_dot(left_rows, right_stack)
        ).astype(jnp.bfloat16)

    kernel_tile = lax.map(kernel_rows, positions).reshape(row_count, col_count)
    row_mass = src_weight / src_mass
    col_mass = tgt_weight / tgt_mass
    col_scale = jnp.ones((col_count,), jnp.float32)
    row_scale = jnp.ones((row_count,), jnp.float32)
    for sweep in range(SWEEPS):
        row_total = taken_together(
            jnp.dot(
                kernel_tile, col_scale.astype(jnp.bfloat16), preferred_element_type=jnp.float32
            ),
            COL,
        )
        row_scale = row_mass / row_total
        col_total = taken_together(
            lax.dot_general(
                kernel_tile,
                row_scale.astype(jnp.bfloat16),
                (((0,), (0,)), ((), ())),
                preferred_element_type=jnp.float32,
            ),
            ROW,
        )
        col_scale = col_mass / col_total
    scaled_right = (tgt_right_full * col_scale[None, :]).astype(jnp.bfloat16)
    closing_side = row_scale[:, None] * lax.dot_general(
        kernel_tile, scaled_right, (((1,), (1,)), ((), ())), preferred_element_type=jnp.float32
    )
    core_local = jnp.dot(right_full.astype(jnp.float32), closing_side, precision=highest)
    new_core = mass_scale * over_axes(core_local, ROW_COL)
    row_potential = jnp.log(row_scale) + math.log(n_all) + math.log(m_all)
    col_potential = jnp.log(col_scale)
    return (row_potential, col_potential, new_core)


def solution(mesh):
    torus = Mesh(mesh.devices.reshape(8, 2, 8, 4), ("row_0", "row_1", "col_0", "col_1"))
    placed = (
        P(COL, ROW),
        P(COL, ROW),
        P(COL, ROW),
        P(ROW),
        P(ROW),
        P(ROW, COL),
        P(ROW, COL),
        P(ROW, COL),
        P(COL),
        P(COL),
    )
    return jax.shard_map(
        body, mesh=torus, in_specs=placed, out_specs=(P(ROW), P(COL), P()), check_vma=False
    )
```

profile of v0, /device:TPU:4, one launch (start us, length us, event | category | flops | bytes accessed | tf_op | source)
XLA Modules:
  0.0 431.6 jit_solution(10800246159475264838)
XLA Ops:
  1.4 19.7 %all-gather.1 = bf16[16,4,6144]{2,1,0:T(4,128)(2,1)S(1)} all-gather(bf16[1,4,6144]{2,1,0:T(4,128)(2,1)S(1)} %maximum_bitcast_fusion), channel_id=1, replica_groups=mesh['row_0'=8,'row_1'=2,'col_0'=8,'col_1'=4] {'row_0','row_1'}, dimensions={0}, use_global_device_ids=true | all-gather | bytes 835584 | tf_op jit(solution)/shard_map/all_gather | solution.py:21
  22.2 55.4 %all-gather = bf16[32,2,6144]{2,1,0:T(2,128)(2,1)S(1)} all-gather(bf16[1,2,6144]{2,1,0:T(2,128)(2,1)S(1)} %maximum_bitcast_fusion.1), channel_id=1, replica_groups=mesh['row_0'=8,'row_1'=2,'col_0'=8,'col_1'=4] {'col_0','col_1'}, dimensions={0}, use_global_device_ids=true | all-gather | bytes 811008 | tf_op jit(solution)/shard_map/all_gather | solution.py:21
  78.0 40.4 %while.22 = (s32[]{:T(128)}, f32[4]{0:T(128)S(1)}, f32[4,512,64]{1,0,2:T(4,128)}, s32[4]{0:T(128)S(1)}, f32[2048]{0:T(1024)}, /*index=5*/f32[2048]{0:T(1024)}, b...) while((s32[]{:T(128)}, f32[4]{0:T(128)S(1)}, ...), condition=%wide.region_7.8_spmd, body=%wide.region_5.7_spmd.sunk | while | flops 273678336 | bytes 5454035 | solution.py:87
  123.1 29.2 %all-reduce.1 = (f32[]{:T(128)}, f32[64,64]{1,0:T(8,128)S(1)}, f32[]{:T(128)}, f32[]{:T(128)}) all-reduce(f32[]{:T(128)} %reduce_sum.91, f32[64,64]{1,0:T(8,128)S(1)} %fusion.11, f32[]{:T(128)S(6)} %div.38, f32[]{:T(128)S(6)} %div.42), channel_id=1, replica_groups=mesh['row_0'=8,'row_1'=2,'col_0'=8,'col_1'=4] {'row_0'}, use_global_device_ids=true, to_apply=%region_13.14 | all-reduce | flops 4099 | bytes 32792 | tf_op jit(solution)/shard_map/psum | solution.py:26
  152.3 4.6 %all-reduce.3 = (f32[]{:T(128)}, f32[64,64]{1,0:T(8,128)S(1)}, f32[]{:T(128)}, f32[]{:T(128)}) all-reduce(f32[]{:T(128)} %get-tuple-element.134, f32[64,64]{1,0:T(8,128)S(1)} %get-tuple-element.135, f32[]{:T(128)} %get-tuple-element.136, f32[]{:T(128)} %get-tuple-element.137), channel_id=1, replica_groups=mesh['row_0'=8,'row_1'=2,'col_0'=8,'col_1'=4] {'row_1'}, use_global_device_ids=true, to_apply=%region_14.15 | all-reduce | flops 4099 | bytes 32792 | tf_op jit(solution)/shard_map/psum | solution.py:26
  156.9 29.7 %all-reduce = (f32[]{:T(128)}, f32[64,64]{1,0:T(8,128)S(1)}, f32[]{:T(128)}, f32[]{:T(128)}) all-reduce(f32[]{:T(128)} %get-tuple-element.142, f32[64,64]{1,0:T(8,128)S(1)} %get-tuple-element.143, f32[]{:T(128)} %get-tuple-element.144, f32[]{:T(128)} %get-tuple-element.145), channel_id=1, replica_groups=mesh['row_0'=8,'row_1'=2,'col_0'=8,'col_1'=4] {'col_0'}, use_global_device_ids=true, to_apply=%region_15.16 | all-reduce | flops 4099 | bytes 32792 | tf_op jit(solution)/shard_map/psum | solution.py:26
  186.6 16.0 %all-reduce.2 = (f32[]{:T(128)}, f32[64,64]{1,0:T(8,128)S(1)}, f32[]{:T(128)}, f32[]{:T(128)}) all-reduce(f32[]{:T(128)} %get-tuple-element.130, f32[64,64]{1,0:T(8,128)S(1)} %get-tuple-element.131, f32[]{:T(128)} %get-tuple-element.132, f32[]{:T(128)} %get-tuple-element.133), channel_id=1, replica_groups=mesh['row_0'=8,'row_1'=2,'col_0'=8,'col_1'=4] {'col_1'}, use_global_device_ids=true, to_apply=%region_16.17 | all-reduce | flops 4099 | bytes 32792 | tf_op jit(solution)/shard_map/psum | solution.py:26
  205.3 21.6 %while.23 = (s32[]{:T(128)}, bf16[4,512,2048]{2,1,0:T(8,128)(2,1)}, s32[4]{0:T(128)S(1)}, f32[2048]{0:T(1024)}, f32[2048]{0:T(1024)}, /*index=5*/f32[]{:T(128)},...) while((s32[]{:T(128)}, bf16[4,512,2048]{2,1,0:T(8,128)(2,1)}, ...), condition=%wide.region_18.19_spmd, body=%wide.region_17.18_spmd.sunk | while | flops 272629760 | bytes 2768055 | solution.py:116
  226.9 5.6 %fusion.17 = f32[1,2048]{1,0:T(1,128)S(1)} fusion(bf16[2048,2048]{1,0:T(8,128)(2,1)} %bitcast.60), kind=kOutput, calls=%fused_computation.37 | convolution fusion | flops 8388608 | bytes 8396800 | tf_op jit(solution)/shard_map/dot_general | solution.py:123
  232.7 15.4 %all_to_all.36 = f32[32,1,2048]{2,1,0:T(1,128)S(1)} all-to-all(f32[32,1,2048]{2,1,0:T(1,128)S(1)} %broadcast_in_dim.34), channel_id=1, replica_groups=mesh['row_0'=8,'row_1'=2,'col_0'=8,'col_1'=4] {'col_0','col_1'}, dimensions={0} | all-to-all | bytes 524288 | tf_op jit(solution)/shard_map/all_to_all | solution.py:32
  248.9 4.6 %fusion.25 = f32[1,2048]{1,0:T(1,128)S(1)} fusion(bf16[2048,2048]{1,0:T(8,128)(2,1)} %bitcast.61, bf16[2048,1]{0,1:T(2,128)(2,1)S(1)} %reshape.66), kind=kOutput, calls=%fused_computation.45 | convolution fusion | flops 8388608 | bytes 8400896 | tf_op jit(solution)/shard_map/dot_general | solution.py:130
  253.5 12.4 %all_to_all.37 = f32[16,1,2048]{2,1,0:T(1,128)S(1)} all-to-all(f32[16,1,2048]{2,1,0:T(1,128)S(1)} %broadcast_in_dim.35), channel_id=1, replica_groups=mesh['row_0'=8,'row_1'=2,'col_0'=8,'col_1'=4] {'row_0','row_1'}, dimensions={0} | all-to-all | bytes 262144 | tf_op jit(solution)/shard_map/all_to_all | solution.py:32
  266.7 5.6 %fusion.26 = f32[1,2048]{1,0:T(1,128)S(1)} fusion(bf16[2048,2048]{1,0:T(8,128)(2,1)} %bitcast.62, bf16[2048,1]{0,1:T(2,128)(2,1)S(1)} %reshape.68), kind=kOutput, calls=%fused_computation.46 | convolution fusion | flops 8388608 | bytes 8400896 | tf_op jit(solution)/shard_map/dot_general | solution.py:123
  272.4 17.4 %all_to_all.38 = f32[32,1,2048]{2,1,0:T(1,128)S(1)} all-to-all(f32[32,1,2048]{2,1,0:T(1,128)S(1)} %broadcast_in_dim.36), channel_id=1, replica_groups=mesh['row_0'=8,'row_1'=2,'col_0'=8,'col_1'=4] {'col_0','col_1'}, dimensions={0} | all-to-all | bytes 524288 | tf_op jit(solution)/shard_map/all_to_all | solution.py:32
  290.7 4.6 %fusion.27 = f32[1,2048]{1,0:T(1,128)S(1)} fusion(bf16[2048,2048]{1,0:T(8,128)(2,1)} %bitcast.63, bf16[2048,1]{0,1:T(2,128)(2,1)S(1)} %reshape.70), kind=kOutput, calls=%fused_computation.47 | convolution fusion | flops 8388608 | bytes 8400896 | tf_op jit(solution)/shard_map/dot_general | solution.py:130
  295.3 11.2 %all_to_all.39 = f32[16,1,2048]{2,1,0:T(1,128)S(1)} all-to-all(f32[16,1,2048]{2,1,0:T(1,128)S(1)} %broadcast_in_dim.37), channel_id=1, replica_groups=mesh['row_0'=8,'row_1'=2,'col_0'=8,'col_1'=4] {'row_0','row_1'}, dimensions={0} | all-to-all | bytes 262144 | tf_op jit(solution)/shard_map/all_to_all | solution.py:32
  307.3 5.6 %fusion.28 = f32[1,2048]{1,0:T(1,128)S(1)} fusion(bf16[2048,2048]{1,0:T(8,128)(2,1)} %bitcast.64, bf16[2048,1]{0,1:T(2,128)(2,1)S(1)} %reshape.72), kind=kOutput, calls=%fused_computation.48 | convolution fusion | flops 8388608 | bytes 8400896 | tf_op jit(solution)/shard_map/dot_general | solution.py:123
  313.1 17.6 %all_to_all.40 = f32[32,1,2048]{2,1,0:T(1,128)S(1)} all-to-all(f32[32,1,2048]{2,1,0:T(1,128)S(1)} %broadcast_in_dim.38), channel_id=1, replica_groups=mesh['row_0'=8,'row_1'=2,'col_0'=8,'col_1'=4] {'col_0','col_1'}, dimensions={0} | all-to-all | bytes 524288 | tf_op jit(solution)/shard_map/all_to_all | solution.py:32
  331.6 4.6 %fusion.29 = f32[1,2048]{1,0:T(1,128)S(1)} fusion(bf16[2048,2048]{1,0:T(8,128)(2,1)} %bitcast.65, bf16[2048,1]{0,1:T(2,128)(2,1)S(1)} %reshape.74), kind=kOutput, calls=%fused_computation.49 | convolution fusion | flops 8388608 | bytes 8400896 | tf_op jit(solution)/shard_map/dot_general | solution.py:130
  341.0 8.0 %all-to-all-done.5 = f32[16,1,2048]{2,1,0:T(1,128)S(1)} async-done(((f32[16,1,2048]{2,1,0:T(1,128)}), f32[16,1,2048]{2,1,0:T(1,128)S(1)}, u32[]{:S(2)}, u32[]{:S(2)}) %all-to-all-start.5) | async-done | bytes 131104 | tf_op jit(solution)/shard_map/all_to_all | solution.py:32
  350.3 6.0 %convolution_multiply_fusion = f32[2048,64]{0,1:T(8,128)S(1)} fusion(bf16[2048,2048]{1,0:T(8,128)(2,1)} %bitcast.66, f32[2048]{0:T(1024)S(1)} %get-tuple-element.147, f32[2048]{0:T(1024)S(1)} %get-tuple-element.149, bf16[64,6144]{1,0:T(8,128)(2,1)S(1)} %reshape.63), kind=kOutput, calls=%fused_computation.10 | convolution fusion | flops 537395200 | bytes 9191424 | tf_op jit(solution)/shard_map/dot_general | solution.py:140
  356.8 27.5 %psum.156 = f32[64,64]{1,0:T(8,128)S(1)} all-reduce(f32[64,64]{1,0:T(8,128)S(1)} %fusion.9), channel_id=1, replica_groups=mesh['row_0'=8,'row_1'=2,'col_0'=8,'col_1'=4] {'row_0'}, use_global_device_ids=true, to_apply=%region_30.31 | all-reduce | flops 4096 | bytes 32768 | tf_op jit(solution)/shard_map/psum | solution.py:26
  387.7 27.5 %psum.158 = f32[64,64]{1,0:T(8,128)S(1)} all-reduce(f32[64,64]{1,0:T(8,128)S(1)} %psum.157), channel_id=1, replica_groups=mesh['row_0'=8,'row_1'=2,'col_0'=8,'col_1'=4] {'col_0'}, use_global_device_ids=true, to_apply=%region_32.33 | all-reduce | flops 4096 | bytes 32768 | tf_op jit(solution)/shard_map/psum | solution.py:26
  415.2 15.8 %psum.159 = f32[64,64]{1,0:T(8,128)S(1)} all-reduce(f32[64,64]{1,0:T(8,128)S(1)} %psum.158), channel_id=1, replica_groups=mesh['row_0'=8,'row_1'=2,'col_0'=8,'col_1'=4] {'col_1'}, use_global_device_ids=true, to_apply=%region_33.34 | all-reduce | flops 4096 | bytes 32768 | tf_op jit(solution)/shard_map/psum | solution.py:26
  (90 shorter events, 79.4 us)
Async XLA Ops:
  78.0 42.6 %copy-start = (f32[2048]{0:T(1024)S(1)}, f32[2048]{0:T(1024)}, u32[]{:S(2)}) copy-start(f32[2048]{0:T(1024)} %param.18) | copy-start | bytes 24580
  78.0 43.2 %copy-start.1 = (f32[2048]{0:T(1024)S(1)}, f32[2048]{0:T(1024)}, u32[]{:S(2)}) copy-start(f32[2048]{0:T(1024)} %param.23) | copy-start | bytes 24580
  336.9 12.1 %all-to-all-start.5 = ((f32[16,1,2048]{2,1,0:T(1,128)}), f32[16,1,2048]{2,1,0:T(1,128)S(1)}, u32[]{:S(2)}, u32[]{:S(2)}) async-start(f32[16,1,2048]{2,1,0:T(1,128)} %broadcast_in_dim.39), calls=%async_computation.5 | async-start | bytes 262144 | tf_op jit(solution)/shard_map/all_to_all | solution.py:32
where the time goes:
time: 434 us; the launch traced here: 432 us
  blocking collectives  303 us (70%)
  matrix products  66.2 us (15%)
  local copies, waits for them, and re-layouts  32.1 us (7%)
  other arithmetic  10.8 us (2%)
  waiting for transfers between devices  8.01 us (2%)
  loops' own time  5.24 us (1%)
    psum x8, blocking collectives, over_axes(): value = lax.psum(value, axis)  154 us
    all_gather x2, blocking collectives, in_one_piece(): lax.all_gather(both, axis, axis=dim, tiled=True)  75.2 us
    all_to_all x5, blocking collectives, sent_to_all(): lax.all_to_all(jnp.broadcast_to(value[None], (peers, *value.shape)), axis...  74 us
    dot_general x8, matrix products, inner_dot(): lax.dot_general(left_side, right_side, (((0,), (0,)), ((), ())), preferre...  24.7 us
    dynamic_update_slice x12, local copies, waits for them, and re-layouts, body(): tile_totals, side_rows = lax.map(opening, positions)  18.1 us
    dot_general x3, matrix products, body(): jnp.dot(kernel_tile, col_scale.astype(jnp.bfloat16), preferred_element_ty...  16.9 us
    dot_general x3, matrix products, body(): lax.dot_general(kernel_tile, row_scale.astype(jnp.bfloat16), (((0,), (0,)...  13.7 us
  transfers between devices with their start and end apart: 1, of which 1 were waited for; matrix products, arithmetic and copies ran while one was open for 0% of the time, Pallas kernels for 0%

commit v1 on v0

--- a/solution.py
+++ b/solution.py
@@ -9,7 +9,6 @@
 SWEEPS = 3
 ROW = ("row_0", "row_1")
 COL = ("col_0", "col_1")
-ROW_COL = ("row_0", "row_1", "col_0", "col_1")
 
 
 def in_one_piece(arrays, axis, dim, along):
@@ -21,12 +20,6 @@
     return tuple(jnp.split(lax.all_gather(both, axis, axis=dim, tiled=True), ends, axis=along))
 
 
-def over_axes(value, axes):
-    for axis in axes:
-        value = lax.psum(value, axis)
-    return value
-
-
 def sent_to_all(value, axis):
     peers = lax.axis_size(axis)
     return lax.all_to_all(
@@ -35,7 +28,13 @@
 
 
 def taken_together(value, axis):
-    return sent_to_all(value, axis).sum(axis=0)
+    received = sent_to_all(value.astype(jnp.bfloat16), axis)
+    return received.astype(jnp.float32).sum(axis=0)
+
+
+def core_over_all(core):
+    flat = core.reshape(-1, 128)
+    return taken_together(taken_together(flat, ROW), COL).reshape(core.shape)
 
 
 def inner_dot(left_side, right_side):
@@ -61,7 +60,9 @@
     col_count = tgt_logit.shape[0]
     n_all = row_count * lax.axis_size(ROW)
     m_all = col_count * lax.axis_size(COL)
-    embed_full, left_full, right_full = in_one_piece((src_embed, src_left, src_right), COL, 0, 1)
+    src_mine = jnp.concatenate((src_embed, src_left, src_right), axis=1)
+    src_full = sent_to_all(src_mine, COL).reshape(-1, src_mine.shape[1])
+    embed_full, left_full, right_full = jnp.split(src_full, 3, axis=1)
     tgt_embed_full, tgt_left_full, tgt_right_full = in_one_piece(
         (tgt_embed, tgt_left, tgt_right), ROW, 0, 1
     )
@@ -88,14 +89,10 @@
     side_sum = side_rows.reshape(row_count, rank_width)
     local_total = jnp.sum(tile_totals)
     core_part = jnp.dot(right_full.astype(jnp.float32), side_sum, precision=highest)
-    src_part = jnp.sum(src_weight) / lax.axis_size(COL)
-    tgt_part = jnp.sum(tgt_weight) / lax.axis_size(ROW)
-    grand_total, core_sum, src_mass, tgt_mass = (
-        over_axes(local_total, ROW_COL),
-        over_axes(core_part, ROW_COL),
-        over_axes(src_part, ROW_COL),
-        over_axes(tgt_part, ROW_COL),
-    )
+    row_sums = sent_to_all(jnp.stack([local_total, jnp.sum(src_weight)]), ROW).sum(axis=0)
+    col_sums = sent_to_all(jnp.stack([row_sums[0], jnp.sum(tgt_weight)]), COL).sum(axis=0)
+    grand_total, src_mass, tgt_mass = col_sums[0], row_sums[1], col_sums[1]
+    core_sum = core_over_all(core_part)
     mass_scale = math.sqrt(n_all * m_all)
     mixing = mass_scale * core_sum / grand_total
     row_factor = (2.0 * jnp.dot(mixing.T, left_full.astype(jnp.float32), precision=highest)).astype(
@@ -141,7 +138,7 @@
         kernel_tile, scaled_right, (((1,), (1,)), ((), ())), preferred_element_type=jnp.float32
     )
     core_local = jnp.dot(right_full.astype(jnp.float32), closing_side, precision=highest)
-    new_core = mass_scale * over_axes(core_local, ROW_COL)
+    new_core = mass_scale * core_over_all(core_local)
     row_potential = jnp.log(row_scale) + math.log(n_all) + math.log(m_all)
     col_potential = jnp.log(col_scale)
     return (row_potential, col_potential, new_core)

time: 434 us -> 313 us (0.72)
  the two profiles are of different devices: /device:TPU:4 before, /device:TPU:1 now
where the time goes in v1:
time: 313 us; the launch traced here: 312 us
  blocking collectives  109 us (35%)
  matrix products  58.7 us (19%)
  waiting for transfers between devices  43.8 us (14%)
  starting transfers between devices  39.4 us (13%)
  local copies, waits for them, and re-layouts  33.8 us (11%)
  other arithmetic  20.5 us (7%)
  loops' own time  5.02 us (2%)
    all_to_all x7, blocking collectives, sent_to_all(): lax.all_to_all(jnp.broadcast_to(value[None], (peers, *value.shape)), axis...  88.3 us
    all_to_all x6, waiting for transfers between devices, sent_to_all(): lax.all_to_all(jnp.broadcast_to(value[None], (peers, *value.shape)), axis...  43.8 us
    all_to_all x6, starting transfers between devices, sent_to_all(): lax.all_to_all(jnp.broadcast_to(value[None], (peers, *value.shape)), axis...  39.4 us
    all_gather x1, blocking collectives, in_one_piece(): lax.all_gather(both, axis, axis=dim, tiled=True)  20.5 us
    dynamic_update_slice x12, local copies, waits for them, and re-layouts, body(): tile_totals, side_rows = lax.map(opening, positions)  18.1 us
    dot_general x8, matrix products, inner_dot(): lax.dot_general(left_side, right_side, (((0,), (0,)), ((), ())), preferre...  17.8 us
    dot_general x3, matrix products, body(): jnp.dot(kernel_tile, col_scale.astype(jnp.bfloat16), preferred_element_ty...  16.9 us
    dot_general x3, matrix products, body(): lax.dot_general(kernel_tile, row_scale.astype(jnp.bfloat16), (((0,), (0,)...  13.7 us
  transfers between devices with their start and end apart: 6, of which 5 were waited for; matrix products, arithmetic and copies ran while one was open for 2% of the time, Pallas kernels for 0%

profile of v1, /device:TPU:1, one launch (start us, length us, event | category | flops | bytes accessed | tf_op | source)
XLA Modules:
  0.0 311.8 jit_solution(17907114439071790497)
XLA Ops:
  2.7 13.7 %all-to-all-start = ((bf16[32,2,6144]{2,1,0:T(2,128)(2,1)}), bf16[32,2,6144]{2,1,0:T(2,128)(2,1)S(1)}, u32[]{:S(2)}, u32[]{:S(2)}) async-start(bf16[32,2,6144]{2,1,0:T(2,128)(2,1)} %broadcast_in_dim.47), calls=%async_computation | async-start | bytes 1572864 | tf_op jit(solution)/shard_map/all_to_all | solution.py:25
  17.2 20.5 %all-gather = bf16[16,4,6144]{2,1,0:T(4,128)(2,1)S(1)} all-gather(bf16[1,4,6144]{2,1,0:T(4,128)(2,1)S(1)} %maximum_bitcast_fusion), channel_id=1, replica_groups=mesh['row_0'=8,'row_1'=2,'col_0'=8,'col_1'=4] {'row_0','row_1'}, dimensions={0}, use_global_device_ids=true | all-gather | bytes 835584 | tf_op jit(solution)/shard_map/all_gather | solution.py:20
  39.7 34.9 %while.22 = (s32[]{:T(128)}, f32[4]{0:T(128)S(1)}, f32[4,512,64]{1,0,2:T(4,128)}, s32[4]{0:T(128)S(1)}, f32[2048]{0:T(1024)S(1)}, /*index=5*/f32[2048]{0:T(1024)...) while((s32[]{:T(128)}, f32[4]{0:T(128)S(1)}, ...), condition=%wide.region_2.3_spmd, body=%wide.region_0.2_spmd.sunk | while | flops 273678336 | bytes 5454035 | solution.py:88
  78.4 8.1 %all-to-all-start.1 = ((f32[16,1,2]{2,1,0:T(1,128)}), f32[16,1,2]{2,1,0:T(1,128)S(1)}, u32[]{:S(2)}, u32[]{:S(2)}) async-start(f32[16,1,2]{2,1,0:T(1,128)} %broadcast_in_dim.48), calls=%async_computation.1 | async-start | bytes 16384 | tf_op jit(solution)/shard_map/all_to_all | solution.py:25
  86.9 6.5 %all-to-all-done.1 = f32[16,1,2]{2,1,0:T(1,128)S(1)} async-done(((f32[16,1,2]{2,1,0:T(1,128)}), f32[16,1,2]{2,1,0:T(1,128)S(1)}, u32[]{:S(2)}, u32[]{:S(2)}) %all-to-all-start.1) | async-done | bytes 160 | tf_op jit(solution)/shard_map/all_to_all | solution.py:25
  100.6 6.6 %all-to-all-done.3 = bf16[16,32,128]{2,1,0:T(8,128)(2,1)S(1)} async-done(((bf16[16,32,128]{2,1,0:T(8,128)(2,1)}), bf16[16,32,128]{2,1,0:T(8,128)(2,1)S(1)}, u32[]{:S(2)}, u32[]{:S(2)}) %all-to-all-start.3) | async-done | bytes 131104 | tf_op jit(solution)/shard_map/all_to_all | solution.py:25
  107.8 5.9 %all-to-all-start.2 = ((f32[32,1,2]{2,1,0:T(1,128)}), f32[32,1,2]{2,1,0:T(1,128)S(1)}, u32[]{:S(2)}, u32[]{:S(2)}) async-start(f32[32,1,2]{2,1,0:T(1,128)} %broadcast_in_dim.50), calls=%async_computation.2 | async-start | bytes 32768 | tf_op jit(solution)/shard_map/all_to_all | solution.py:25
  113.8 8.5 %all-to-all-done.2 = f32[32,1,2]{2,1,0:T(1,128)S(1)} async-done(((f32[32,1,2]{2,1,0:T(1,128)}), f32[32,1,2]{2,1,0:T(1,128)S(1)}, u32[]{:S(2)}, u32[]{:S(2)}) %all-to-all-start.2) | async-done | bytes 288 | tf_op jit(solution)/shard_map/all_to_all | solution.py:25
  128.2 9.9 %all-to-all-done.4 = bf16[32,32,128]{2,1,0:T(8,128)(2,1)S(1)} async-done(((bf16[32,32,128]{2,1,0:T(8,128)(2,1)}), bf16[32,32,128]{2,1,0:T(8,128)(2,1)S(1)}, u32[]{:S(2)}, u32[]{:S(2)}) %all-to-all-start.4) | async-done | bytes 262176 | tf_op jit(solution)/shard_map/all_to_all | solution.py:25
  139.4 14.2 %while.23 = (s32[]{:T(128)}, bf16[4,512,2048]{2,1,0:T(8,128)(2,1)}, s32[4]{0:T(128)S(1)}, f32[2048]{0:T(1024)S(1)}, f32[2048]{0:T(1024)S(1)}, /*index=5*/f32[]{:...) while((s32[]{:T(128)}, bf16[4,512,2048]{2,1,0:T(8,128)(2,1)}, ...), condition=%wide.region_11.12_spmd, body=%wide.region_10.11_spmd.sunk | while | flops 272629760 | bytes 2768055 | solution.py:113
  153.6 5.7 %fusion.11 = f32[1,2048]{1,0:T(1,128)S(1)} fusion(bf16[2048,2048]{1,0:T(8,128)(2,1)} %bitcast.65), kind=kOutput, calls=%fused_computation.42 | convolution fusion | flops 8388608 | bytes 8396800 | tf_op jit(solution)/shard_map/dot_general | solution.py:120
  161.4 13.9 %all_to_all.73 = bf16[32,2,1024]{2,1,0:T(2,128)(2,1)S(1)} all-to-all(bf16[32,2,1024]{2,1,0:T(2,128)(2,1)S(1)} %reshape.121), channel_id=1, replica_groups=mesh['row_0'=8,'row_1'=2,'col_0'=8,'col_1'=4] {'col_0','col_1'}, dimensions={0} | all-to-all | bytes 262144 | tf_op jit(solution)/shard_map/all_to_all | solution.py:25
  176.1 4.6 %fusion.20 = f32[1,2048]{1,0:T(1,128)S(1)} fusion(bf16[2048,2048]{1,0:T(8,128)(2,1)} %bitcast.66, bf16[2048,1]{0,1:T(2,128)(2,1)S(1)} %reshape.111), kind=kOutput, calls=%fused_computation.53 | convolution fusion | flops 8388608 | bytes 8400896 | tf_op jit(solution)/shard_map/dot_general | solution.py:127
  181.8 13.3 %all_to_all.74 = bf16[16,2,1024]{2,1,0:T(2,128)(2,1)S(1)} all-to-all(bf16[16,2,1024]{2,1,0:T(2,128)(2,1)S(1)} %reshape.123), channel_id=1, replica_groups=mesh['row_0'=8,'row_1'=2,'col_0'=8,'col_1'=4] {'row_0','row_1'}, dimensions={0} | all-to-all | bytes 131072 | tf_op jit(solution)/shard_map/all_to_all | solution.py:25
  195.9 5.6 %fusion.21 = f32[1,2048]{1,0:T(1,128)S(1)} fusion(bf16[2048,2048]{1,0:T(8,128)(2,1)} %bitcast.67, bf16[2048,1]{0,1:T(2,128)(2,1)S(1)} %reshape.113), kind=kOutput, calls=%fused_computation.54 | convolution fusion | flops 8388608 | bytes 8400896 | tf_op jit(solution)/shard_map/dot_general | solution.py:120
  203.2 12.8 %all_to_all.75 = bf16[32,2,1024]{2,1,0:T(2,128)(2,1)S(1)} all-to-all(bf16[32,2,1024]{2,1,0:T(2,128)(2,1)S(1)} %reshape.125), channel_id=1, replica_groups=mesh['row_0'=8,'row_1'=2,'col_0'=8,'col_1'=4] {'col_0','col_1'}, dimensions={0} | all-to-all | bytes 262144 | tf_op jit(solution)/shard_map/all_to_all | solution.py:25
  216.9 4.6 %fusion.22 = f32[1,2048]{1,0:T(1,128)S(1)} fusion(bf16[2048,2048]{1,0:T(8,128)(2,1)} %bitcast.68, bf16[2048,1]{0,1:T(2,128)(2,1)S(1)} %reshape.115), kind=kOutput, calls=%fused_computation.55 | convolution fusion | flops 8388608 | bytes 8400896 | tf_op jit(solution)/shard_map/dot_general | solution.py:127
  222.6 11.9 %all_to_all.76 = bf16[16,2,1024]{2,1,0:T(2,128)(2,1)S(1)} all-to-all(bf16[16,2,1024]{2,1,0:T(2,128)(2,1)S(1)} %reshape.127), channel_id=1, replica_groups=mesh['row_0'=8,'row_1'=2,'col_0'=8,'col_1'=4] {'row_0','row_1'}, dimensions={0} | all-to-all | bytes 131072 | tf_op jit(solution)/shard_map/all_to_all | solution.py:25
  235.3 5.6 %fusion.23 = f32[1,2048]{1,0:T(1,128)S(1)} fusion(bf16[2048,2048]{1,0:T(8,128)(2,1)} %bitcast.69, bf16[2048,1]{0,1:T(2,128)(2,1)S(1)} %reshape.117), kind=kOutput, calls=%fused_computation.56 | convolution fusion | flops 8388608 | bytes 8400896 | tf_op jit(solution)/shard_map/dot_general | solution.py:120
  242.6 12.8 %all_to_all.77 = bf16[32,2,1024]{2,1,0:T(2,128)(2,1)S(1)} all-to-all(bf16[32,2,1024]{2,1,0:T(2,128)(2,1)S(1)} %reshape.129), channel_id=1, replica_groups=mesh['row_0'=8,'row_1'=2,'col_0'=8,'col_1'=4] {'col_0','col_1'}, dimensions={0} | all-to-all | bytes 262144 | tf_op jit(solution)/shard_map/all_to_all | solution.py:25
  261.9 11.9 %all_to_all.78 = bf16[16,2,1024]{2,1,0:T(2,128)(2,1)S(1)} all-to-all(bf16[16,2,1024]{2,1,0:T(2,128)(2,1)S(1)} %reshape.131), channel_id=1, replica_groups=mesh['row_0'=8,'row_1'=2,'col_0'=8,'col_1'=4] {'row_0','row_1'}, dimensions={0} | all-to-all | bytes 131072 | tf_op jit(solution)/shard_map/all_to_all | solution.py:25
  275.2 6.0 %convolution_multiply_fusion = f32[2048,64]{0,1:T(8,128)S(1)} fusion(bf16[2048,2048]{1,0:T(8,128)(2,1)} %bitcast.71, f32[2048]{0:T(1024)S(1)} %get-tuple-element.131, f32[2048]{0:T(1024)S(1)} %get-tuple-element.133, bf16[64,6144]{1,0:T(8,128)(2,1)S(1)} %reshape.108), kind=kOutput, calls=%fused_computation.10 | convolution fusion | flops 537395200 | bytes 9191424 | tf_op jit(solution)/shard_map/dot_general | solution.py:137
  281.8 11.8 %all_to_all.79 = bf16[16,32,128]{2,1,0:T(8,128)(2,1)S(1)} all-to-all(bf16[16,32,128]{2,1,0:T(8,128)(2,1)S(1)} %broadcast_in_dim.59), channel_id=1, replica_groups=mesh['row_0'=8,'row_1'=2,'col_0'=8,'col_1'=4] {'row_0','row_1'}, dimensions={0} | all-to-all | bytes 262144 | tf_op jit(solution)/shard_map/all_to_all | solution.py:25
  298.8 12.2 %all-to-all-done.12 = bf16[32,32,128]{2,1,0:T(8,128)(2,1)S(1)} async-done(((bf16[32,32,128]{2,1,0:T(8,128)(2,1)}), bf16[32,32,128]{2,1,0:T(8,128)(2,1)S(1)}, u32[]{:S(2)}, u32[]{:S(2)}) %all-to-all-start.12) | async-done | bytes 262176 | tf_op jit(solution)/shard_map/all_to_all | solution.py:25
  (144 shorter events, 92.6 us)
Async XLA Ops:
  0.6 39.0 %copy-start.2 = (f32[2048]{0:T(1024)S(1)}, f32[2048]{0:T(1024)}, u32[]{:S(2)}) copy-start(f32[2048]{0:T(1024)} %param.17) | copy-start | bytes 24580
  0.6 39.0 %copy-start.3 = (f32[2048]{0:T(1024)S(1)}, f32[2048]{0:T(1024)}, u32[]{:S(2)}) copy-start(f32[2048]{0:T(1024)} %param.22) | copy-start | bytes 24580
  2.7 36.6 %all-to-all-start = ((bf16[32,2,6144]{2,1,0:T(2,128)(2,1)}), bf16[32,2,6144]{2,1,0:T(2,128)(2,1)S(1)}, u32[]{:S(2)}, u32[]{:S(2)}) async-start(bf16[32,2,6144]{2,1,0:T(2,128)(2,1)} %broadcast_in_dim.47), calls=%async_computation | async-start | bytes 1572864 | tf_op jit(solution)/shard_map/all_to_all | solution.py:25
  39.7 58.4 %copy-start.1 = (f32[2048]{0:T(1024)S(1)}, f32[2048]{0:T(1024)}, u32[]{:S(2)}) copy-start(f32[2048]{0:T(1024)} %param.23) | copy-start | bytes 24580
  78.4 15.0 %all-to-all-start.1 = ((f32[16,1,2]{2,1,0:T(1,128)}), f32[16,1,2]{2,1,0:T(1,128)S(1)}, u32[]{:S(2)}, u32[]{:S(2)}) async-start(f32[16,1,2]{2,1,0:T(1,128)} %broadcast_in_dim.48), calls=%async_computation.1 | async-start | bytes 16384 | tf_op jit(solution)/shard_map/all_to_all | solution.py:25
  94.1 13.1 %all-to-all-start.3 = ((bf16[16,32,128]{2,1,0:T(8,128)(2,1)}), bf16[16,32,128]{2,1,0:T(8,128)(2,1)S(1)}, u32[]{:S(2)}, u32[]{:S(2)}) async-start(bf16[16,32,128]{2,1,0:T(8,128)(2,1)} %broadcast_in_dim.51), calls=%async_computation.3 | async-start | bytes 262144 | tf_op jit(solution)/shard_map/all_to_all | solution.py:25
  107.8 14.5 %all-to-all-start.2 = ((f32[32,1,2]{2,1,0:T(1,128)}), f32[32,1,2]{2,1,0:T(1,128)S(1)}, u32[]{:S(2)}, u32[]{:S(2)}) async-start(f32[32,1,2]{2,1,0:T(1,128)} %broadcast_in_dim.50), calls=%async_computation.2 | async-start | bytes 32768 | tf_op jit(solution)/shard_map/all_to_all | solution.py:25
  123.1 15.1 %all-to-all-start.4 = ((bf16[32,32,128]{2,1,0:T(8,128)(2,1)}), bf16[32,32,128]{2,1,0:T(8,128)(2,1)S(1)}, u32[]{:S(2)}, u32[]{:S(2)}) async-start(bf16[32,32,128]{2,1,0:T(8,128)(2,1)} %broadcast_in_dim.52), calls=%async_computation.4 | async-start | bytes 524288 | tf_op jit(solution)/shard_map/all_to_all | solution.py:25
  153.6 21.9 %copy-start = (f32[2048]{0:T(1024)S(1)}, f32[2048]{0:T(1024)}, u32[]{:S(2)}) copy-start(f32[2048]{0:T(1024)} %param.18) | copy-start | bytes 24580
  294.3 16.7 %all-to-all-start.12 = ((bf16[32,32,128]{2,1,0:T(8,128)(2,1)}), bf16[32,32,128]{2,1,0:T(8,128)(2,1)S(1)}, u32[]{:S(2)}, u32[]{:S(2)}) async-start(bf16[32,32,128]{2,1,0:T(8,128)(2,1)} %broadcast_in_dim.60), calls=%async_computation.12 | async-start | bytes 524288 | tf_op jit(solution)/shard_map/all_to_all | solution.py:25

commit v2 on v1

v2 whole, which is shorter than its diff:
```python
import functools
import math

import jax
import jax.numpy as jnp
from jax import lax
from jax.experimental import pallas as pl
from jax.experimental.pallas import tpu as pltpu
from jax.sharding import Mesh
from jax.sharding import PartitionSpec as P

SWEEPS = 3
ROW = ("row_0", "row_1")
COL = ("col_0", "col_1")
F32 = jnp.float32
BF16 = jnp.bfloat16
LANES = 128
BLOCK = 256
PAD = 16

VMEM = pl.BlockSpec(memory_space=pltpu.VMEM)
CONTRACT_FIRST = (((0,), (0,)), ((), ()))
CONTRACT_LAST = (((1,), (1,)), ((), ()))
PLAIN = (((1,), (0,)), ((), ()))


def dot(a, b, dims):
    return lax.dot_general(a, b, dims, preferred_element_type=F32)


def three_parts(v):
    high = v.astype(BF16).astype(F32)
    rest = v - high
    mid = rest.astype(BF16).astype(F32)
    low = (rest - mid).astype(BF16).astype(F32)
    return high, mid, low


def logit_rows(v, first):
    n = v.shape[1]
    row = lax.broadcasted_iota(jnp.int32, (PAD, n), 0)
    at, ones = (0, 3) if first else (3, 0)
    out = jnp.where((row >= ones) & (row < ones + 3), 1.0, 0.0)
    for index, part in enumerate(three_parts(v)):
        out = jnp.where(row == at + index, jnp.broadcast_to(part, (PAD, n)), out)
    return out.astype(BF16)


def to_lanes(v, flat_ref):
    for s in range(v.shape[0]):
        flat_ref[:, s * LANES : (s + 1) * LANES] = jnp.broadcast_to(v[s : s + 1], (8, LANES))
    return flat_ref[...]


def to_tiles(row, tile_ref):
    for s in range(tile_ref.shape[0]):
        tile_ref[s : s + 1, :] = row[:, s * LANES : (s + 1) * LANES]
    return tile_ref[...]


def send(out_ref, v):
    v = v.astype(out_ref.dtype)
    for p in range(out_ref.shape[0]):
        out_ref[p] = v


def received(ref):
    total = ref[0].astype(F32)
    for p in range(1, ref.shape[0]):
        total = total + ref[p].astype(F32)
    return total


def halves_on_lanes(core, rank):
    half = rank // 2
    lane = lax.broadcasted_iota(jnp.int32, (half, 2 * rank), 1)
    return jnp.where(lane < rank, core[:half], core[half:rank])


def opening_kernel(src, tgt, src_logit, tgt_logit, src_weight, tgt_weight, out, xs, xt, right, acc):
    rank = src.shape[0]
    n = src_logit.shape[1]
    m = tgt_logit.shape[1]
    xs[:rank] = (src[:, :n].astype(F32) * 0.125).astype(BF16)
    xs[rank:] = logit_rows(src_logit[...], True)
    xt[:rank] = tgt[:, :m]
    xt[rank:] = logit_rows(tgt_logit[...], False)
    right[:rank] = tgt[:, 2 * m :]
    right[rank : 2 * rank] = tgt[:, 2 * m :]
    row = lax.broadcasted_iota(jnp.int32, (PAD, m), 0)
    right[2 * rank :] = jnp.where(row == 0, 1.0, 0.0).astype(BF16)
    acc[...] = jnp.zeros_like(acc)
    one_row = jnp.where(
        lax.broadcasted_iota(jnp.int32, (PAD, BLOCK), 0) == 0, 1.0, 0.0
    ).astype(BF16)

    def step(b, carry):
        at = pl.multiple_of(b * BLOCK, BLOCK)
        x = dot(xs[:, pl.ds(at, BLOCK)], xt[...], CONTRACT_FIRST)
        tile = jnp.exp(x).astype(BF16)
        side = dot(tile, right[...], CONTRACT_LAST)
        left = jnp.concatenate([src[:, pl.ds(2 * n + at, BLOCK)], one_row], axis=0)
        for part in three_parts(side):
            acc[...] += dot(left, part.astype(BF16), PLAIN)
        return carry

    lax.fori_loop(0, n // BLOCK, step, 0)
    core = halves_on_lanes(acc[:, : 2 * rank], rank)
    total = acc[rank : rank + 1, 2 * rank : 2 * rank + 1]
    src_sum = jnp.sum(src_weight[...], keepdims=True)
    tgt_sum = jnp.sum(tgt_weight[...], keepdims=True)
    lane = lax.broadcasted_iota(jnp.int32, (8, LANES), 1)
    sums = jnp.where(lane == 0, total, jnp.where(lane == 1, src_sum, jnp.where(lane == 2, tgt_sum, 0.0)))
    send(out, jnp.concatenate([core, sums], axis=0))


def relay_kernel(y, out):
    send(out, received(y))


def tile_kernel(
    mass_scale, row_peers, col_peers,
    z, src, tgt, src_logit, tgt_logit, src_weight, tgt_weight,
    kernel, out, row_mass, col_mass, xs, xt, totals, tiles,
):
    rank = src.shape[0]
    half = rank // 2
    n = src_logit.shape[1]
    m = tgt_logit.shape[1]
    sums = received(z)
    grand_total = sums[half : half + 1, 0:1]
    row_mass[...] = src_weight[...] / (sums[half : half + 1, 1:2] / col_peers)
    col_mass[...] = tgt_weight[...] / (sums[half : half + 1, 2:3] / row_peers)
    mixing = mass_scale * sums[:half] / grand_total
    parts = jnp.concatenate(three_parts(mixing), axis=0).astype(BF16)
    top = src[:half, n : 2 * n]
    bottom = src[half:, n : 2 * n]
    top = dot(parts, jnp.concatenate([top, top, top], axis=0), CONTRACT_FIRST)
    bottom = dot(parts, jnp.concatenate([bottom, bottom, bottom], axis=0), CONTRACT_FIRST)
    xs[:rank] = (src[:, :n].astype(F32) * 0.125).astype(BF16)
    xs[rank : 2 * rank] = (2.0 * (top[:rank] + bottom[rank:])).astype(BF16)
    xs[2 * rank :] = logit_rows(src_logit[...], True)
    xt[:rank] = tgt[:, :m]
    xt[rank : 2 * rank] = tgt[:, m : 2 * m]
    xt[2 * rank :] = logit_rows(tgt_logit[...] - jnp.log(grand_total), False)
    ones = jnp.ones((PAD, m), BF16)

    def step(b, carry):
        at = pl.multiple_of(b * BLOCK, BLOCK)
        x = dot(xs[:, pl.ds(at, BLOCK)], xt[...], CONTRACT_FIRST)
        tile = jnp.exp(x).astype(BF16)
        kernel[pl.ds(at, BLOCK), :] = tile
        totals[:, pl.ds(at, BLOCK)] = dot(ones, tile, CONTRACT_LAST)[:8]
        return carry

    lax.fori_loop(0, n // BLOCK, step, 0)
    send(out, to_tiles(totals[0:1, :], tiles))


def sweep_kernel(over_rows, y, mass, kernel, scale, out, flat, tiles):
    s = mass[...] / received(y)
    scale[...] = s
    weights = to_lanes(s, flat).astype(BF16)
    total = dot(weights, kernel[...], PLAIN if over_rows else CONTRACT_LAST)
    send(out, to_tiles(total[0:1], tiles))


def closing_kernel(
    shift, y, mass, row_scale, kernel, src, tgt, row_potential, col_potential, out, flat, twice, closing
):
    rank = src.shape[0]
    n, m = kernel.shape
    col_scale = mass[...] / received(y)
    col_potential[...] = jnp.log(col_scale)
    row_potential[...] = jnp.log(row_scale[...]) + shift
    cols = to_lanes(col_scale, flat)
    scaled = (tgt[:, 2 * m :].astype(F32) * cols[0:1]).astype(BF16)
    twice[:rank] = scaled
    twice[rank:] = scaled
    closing[...] = dot(kernel[...], twice[...], CONTRACT_LAST)
    rows = to_lanes(row_scale[...], flat)
    left = src[:, 2 * n :].astype(F32) * rows[0:1]
    core = lax.dot_general(
        left, closing[...], PLAIN, precision=lax.Precision.HIGHEST, preferred_element_type=F32
    )
    send(out, halves_on_lanes(core, rank))


def final_kernel(mass_scale, y, out):
    out[...] = mass_scale * received(y)


def call(body, outs, scratch, *args):
    return pl.pallas_call(
        body,
        out_shape=[jax.ShapeDtypeStruct(s, d) for s, d in outs],
        in_specs=[VMEM] * len(args),
        out_specs=[VMEM] * len(outs),
        scratch_shapes=[pltpu.VMEM(s, d) for s, d in scratch],
        compiler_params=pltpu.CompilerParams(vmem_limit_bytes=24 << 20),
    )(*args)


def exchange(value, axis):
    return lax.all_to_all(value, axis, 0, 0, tiled=True)


def body(
    src_embed,
    src_left,
    src_right,
    src_logit,
    src_weight,
    tgt_embed,
    tgt_left,
    tgt_right,
    tgt_logit,
    tgt_weight,
):
    n, m = src_logit.shape[0], tgt_logit.shape[0]
    row_peers, col_peers = lax.axis_size(ROW), lax.axis_size(COL)
    n_all, m_all = n * row_peers, m * col_peers
    rank = src_embed.shape[0] * col_peers
    half = rank // 2
    mass_scale = math.sqrt(n_all * m_all)
    nt, mt = n // LANES, m // LANES

    mine = jnp.concatenate((src_embed, src_left, src_right), axis=1)
    src = exchange(jnp.broadcast_to(mine[None], (col_peers, *mine.shape)), COL).reshape(rank, 3 * n)
    mine = jnp.concatenate((tgt_embed, tgt_left, tgt_right), axis=1)
    tgt = lax.all_gather(mine, ROW, axis=0, tiled=True)
    src_logit, tgt_logit = src_logit.reshape(1, n), tgt_logit.reshape(1, m)
    src_weight, tgt_weight = src_weight.reshape(nt, LANES), tgt_weight.reshape(mt, LANES)

    (part,) = call(
        opening_kernel,
        [((row_peers, half + 8, LANES), F32)],
        [
            ((rank + PAD, n), BF16),
            ((rank + PAD, m), BF16),
            ((2 * rank + PAD, m), BF16),
            ((rank + PAD, 2 * rank + PAD), F32),
        ],
        src, tgt, src_logit, tgt_logit, src_weight, tgt_weight,
    )
    (part,) = call(relay_kernel, [((col_peers, half + 8, LANES), F32)], [], exchange(part, ROW))
    kernel, part, row_mass, col_mass = call(
        functools.partial(tile_kernel, mass_scale, row_peers, col_peers),
        [
            ((n, m), BF16),
            ((col_peers, nt, LANES), BF16),
            ((nt, LANES), F32),
            ((mt, LANES), F32),
        ],
        [
            ((2 * rank + PAD, n), BF16),
            ((2 * rank + PAD, m), BF16),
            ((8, n), F32),
            ((nt, LANES), F32),
        ],
        exchange(part, COL), src, tgt, src_logit, tgt_logit, src_weight, tgt_weight,
    )
    for sweep in range(SWEEPS):
        row_scale, part = call(
            functools.partial(sweep_kernel, True),
            [((nt, LANES), F32), ((row_peers, mt, LANES), BF16)],
            [((8, n), F32), ((mt, LANES), F32)],
            exchange(part, COL), row_mass, kernel,
        )
        part = exchange(part, ROW)
        if sweep + 1 < SWEEPS:
            _, part = call(
                functools.partial(sweep_kernel, False),
                [((mt, LANES), F32), ((col_peers, nt, LANES), BF16)],
                [((8, m), F32), ((nt, LANES), F32)],
                part, col_mass, kernel,
            )
    row_potential, col_potential, part = call(
        functools.partial(closing_kernel, math.log(n_all) + math.log(m_all)),
        [((nt, LANES), F32), ((mt, LANES), F32), ((row_peers, half, LANES), BF16)],
        [((8, max(n, m)), F32), ((2 * rank, m), BF16), ((n, 2 * rank), F32)],
        part, col_mass, row_scale, kernel, src, tgt,
    )
    (part,) = call(relay_kernel, [((col_peers, half, LANES), BF16)], [], exchange(part, ROW))
    (core,) = call(
        functools.partial(final_kernel, mass_scale), [((half, LANES), F32)], [], exchange(part, COL)
    )
    new_core = jnp.concatenate([core[:, :rank], core[:, rank:]], axis=0)
    return (row_potential.reshape(n), col_potential.reshape(m), new_core)


def solution(mesh):
    torus = Mesh(mesh.devices.reshape(8, 2, 8, 4), ("row_0", "row_1", "col_0", "col_1"))
    placed = (
        P(COL, ROW),
        P(COL, ROW),
        P(COL, ROW),
        P(ROW),
        P(ROW),
        P(ROW, COL),
        P(ROW, COL),
        P(ROW, COL),
        P(COL),
        P(COL),
    )
    return jax.shard_map(
        body, mesh=torus, in_specs=placed, out_specs=(P(ROW), P(COL), P()), check_vma=False
    )
```

time: 313 us -> 223 us (0.71)
  blocking collectives: 109 us -> 170 us
  matrix products: 58.7 us -> 0 us
  waiting for transfers between devices: 43.8 us -> 0.01 us
  Pallas kernels: 0 us -> 30.5 us
  local copies, waits for them, and re-layouts: 33.8 us -> 4.66 us
  starting transfers between devices: 39.4 us -> 13.7 us
  other arithmetic: 20.5 us -> 2.17 us
  loops' own time: 5.02 us -> 0 us
    all_to_all x7 -> x10, blocking collectives: 88.3 us -> 150 us  [exchange(): return lax.all_to_all(value, axis, 0, 0, tiled=True)]
    dot_general x22 -> x0, matrix products: 58.7 us -> none  [the longest x8 17.8 us: inner_dot(): lax.dot_general(left_side, right_side, (((0,), (0,)), ((), ())), preferre...]
    all_to_all x6 -> x1, waiting for transfers between devices: 43.8 us -> 0.01 us  [exchange(): return lax.all_to_all(value, axis, 0, 0, tiled=True)]
    pallas_call x0 -> x11, Pallas kernels: none -> 30.5 us  [call(): pl.pallas_call(body, out_shape=[jax.ShapeDtypeStruct(s, d) for s, d in ou...]
    all_to_all x6 -> x1, starting transfers between devices: 39.4 us -> 13.7 us  [exchange(): return lax.all_to_all(value, axis, 0, 0, tiled=True)]
    dynamic_update_slice x12 -> x0, local copies, waits for them, and re-layouts: 18.1 us -> none  [body(): tile_totals, side_rows = lax.map(opening, positions)]
    broadcast_in_dim x8 -> x0, other arithmetic: 7.14 us -> none  [the longest x6 7.14 us: sent_to_all(): jnp.broadcast_to(value[None], (peers, *value.shape))]
    dynamic_slice x16 -> x0, local copies, waits for them, and re-layouts: 5.19 us -> none  [the longest x8 4.56 us: body(): tile_totals, side_rows = lax.map(opening, positions)]
  transfers between devices with their start and end apart: 6 -> 1, of which waited for: 5 -> 0; matrix products, arithmetic and copies ran while one was open for 2% -> 0% of each run, Pallas kernels for 0% -> 0%
where the time goes in v2:
time: 223 us; the launch traced here: 222 us
  blocking collectives  170 us (76%)
  Pallas kernels  30.5 us (14%)
  starting transfers between devices  13.7 us (6%)
  local copies, waits for them, and re-layouts  4.66 us (2%)
    all_to_all x10, blocking collectives, exchange(): return lax.all_to_all(value, axis, 0, 0, tiled=True)  150 us
    pallas_call x11, Pallas kernels, call(): pl.pallas_call(body, out_shape=[jax.ShapeDtypeStruct(s, d) for s, d in ou...  30.5 us
    all_gather x1, blocking collectives, body(): tgt = lax.all_gather(mine, ROW, axis=0, tiled=True)  20.5 us
    all_to_all x1, starting transfers between devices, exchange(): return lax.all_to_all(value, axis, 0, 0, tiled=True)  13.7 us
  transfers between devices with their start and end apart: 1, of which 0 were waited for; matrix products, arithmetic and copies ran while one was open for 0% of the time, Pallas kernels for 0%

profile of v2, /device:TPU:1, one launch (start us, length us, event | category | flops | bytes accessed | tf_op | source)
XLA Modules:
  0.0 222.3 jit_solution(466056375273633558)
XLA Ops:
  0.7 0.8 pad_maximum_fusion.1
  1.5 1.3 broadcast_in_dim.2
  2.8 13.7 %all-to-all-start = ((bf16[32,2,6144]{2,1,0:T(2,128)(2,1)}), bf16[32,2,6144]{2,1,0:T(2,128)(2,1)S(1)}, u32[]{:S(2)}, u32[]{:S(2)}) async-start(bf16[32,2,6144]{2,1,0:T(2,128)(2,1)} %broadcast_in_dim.2), calls=%async_computation | async-start | bytes 1572864 | tf_op jit(solution)/shard_map/all_to_all | solution.py:205
  16.5 0.8 maximum_bitcast_fusion
  17.3 20.5 %all-gather = bf16[16,4,6144]{2,1,0:T(4,128)(2,1)S(1)} all-gather(bf16[1,4,6144]{2,1,0:T(4,128)(2,1)S(1)} %maximum_bitcast_fusion), channel_id=1, replica_groups=mesh['row_0'=8,'row_1'=2,'col_0'=8,'col_1'=4] {'row_0','row_1'}, dimensions={0}, use_global_device_ids=true | all-gather | bytes 835584 | tf_op jit(solution)/shard_map/all_gather | solution.py:231
  39.0 0.7 copy-done.2
  41.1 8.8 %shard_map.121 = f32[16,40,128]{2,1,0:T(8,128)S(1)} custom-call(bf16[64,6144]{1,0:T(8,128)(2,1)S(1)} %reshape.28.src, bf16[64,6144]{1,0:T(8,128)(2,1)S(1)} %reshape.36.tgt, f32[1,2048]{1,0:T(1,128)S(1)} %bitcast.8, f32[1,2048]{1,0:T(1,128)S(1)} %bitcast.10, f32[16,128]{1,0:T(8,128)S(1)} %bitcast.12, f32[16,128]{1,0:T(8,128)S(1)} %bitcast.14), custom_call_target="tpu_custom_call" | custom-call | tf_op jit(solution)/shard_map/pallas_call | solution.py:194
  49.9 22.2 %all_to_all.55.y = f32[16,40,128]{2,1,0:T(8,128)S(1)} all-to-all(f32[16,40,128]{2,1,0:T(8,128)S(1)} %shard_map.121), channel_id=1, replica_groups=mesh['row_0'=8,'row_1'=2,'col_0'=8,'col_1'=4] {'row_0','row_1'}, dimensions={0} | all-to-all | bytes 655360 | tf_op jit(solution)/shard_map/all_to_all | solution.py:205
  72.1 24.5 %all_to_all.56.z = f32[32,40,128]{2,1,0:T(8,128)S(1)} all-to-all(f32[32,40,128]{2,1,0:T(8,128)S(1)} %shard_map.122), channel_id=1, replica_groups=mesh['row_0'=8,'row_1'=2,'col_0'=8,'col_1'=4] {'col_0','col_1'}, dimensions={0} | all-to-all | bytes 1310720 | tf_op jit(solution)/shard_map/all_to_all | solution.py:205
  96.7 7.7 %shard_map.123 = (bf16[2048,2048]{1,0:T(8,128)(2,1)S(1)}, bf16[32,16,128]{2,1,0:T(8,128)(2,1)S(1)}, f32[16,128]{1,0:T(8,128)S(1)}, f32[16,128]{1,0:T(8,128)S(1)}) custom-call(f32[32,40,128]{2,1,0:T(8,128)S(1)} %all_to_all.56.z, bf16[64,6144]{1,0:T(8,128)(2,1)S(1)} %reshape.28.src, bf16[64,6144]{1,0:T(8,128)(2,1)S(1)} %reshape.36.tgt, f32[1,2048]{1,0:T(1,128)S(1)} %bitcast.9, ...), custom_call_target="tpu_custom_call" | custom-call | tf_op jit(solution)/shard_map/pallas_call | solution.py:194
  104.4 14.2 %all_to_all.57.y = bf16[32,16,128]{2,1,0:T(8,128)(2,1)S(1)} all-to-all(bf16[32,16,128]{2,1,0:T(8,128)(2,1)S(1)} %get-tuple-element.16), channel_id=1, replica_groups=mesh['row_0'=8,'row_1'=2,'col_0'=8,'col_1'=4] {'col_0','col_1'}, dimensions={0} | all-to-all | bytes 262144 | tf_op jit(solution)/shard_map/all_to_all | solution.py:205
  118.5 1.7 shard_map.124
  120.2 12.8 %all_to_all.58.y = bf16[16,16,128]{2,1,0:T(8,128)(2,1)S(1)} all-to-all(bf16[16,16,128]{2,1,0:T(8,128)(2,1)S(1)} %get-tuple-element.19), channel_id=1, replica_groups=mesh['row_0'=8,'row_1'=2,'col_0'=8,'col_1'=4] {'row_0','row_1'}, dimensions={0} | all-to-all | bytes 131072 | tf_op jit(solution)/shard_map/all_to_all | solution.py:205
  133.0 2.7 %shard_map.125 = (f32[16,128]{1,0:T(8,128)}, bf16[32,16,128]{2,1,0:T(8,128)(2,1)S(1)}) custom-call(bf16[16,16,128]{2,1,0:T(8,128)(2,1)S(1)} %all_to_all.58.y, f32[16,128]{1,0:T(8,128)S(1)} %get-tuple-element.20.mass, bf16[2048,2048]{1,0:T(8,128)(2,1)S(1)} %get-tuple-element.18.kernel), custom_call_target="tpu_custom_call" | custom-call | tf_op jit(solution)/shard_map/pallas_call | solution.py:194
  135.7 12.8 %all_to_all.59.y = bf16[32,16,128]{2,1,0:T(8,128)(2,1)S(1)} all-to-all(bf16[32,16,128]{2,1,0:T(8,128)(2,1)S(1)} %get-tuple-element.21), channel_id=1, replica_groups=mesh['row_0'=8,'row_1'=2,'col_0'=8,'col_1'=4] {'col_0','col_1'}, dimensions={0} | all-to-all | bytes 262144 | tf_op jit(solution)/shard_map/all_to_all | solution.py:205
  148.5 1.7 shard_map.126
  150.2 11.7 %all_to_all.60.y = bf16[16,16,128]{2,1,0:T(8,128)(2,1)S(1)} all-to-all(bf16[16,16,128]{2,1,0:T(8,128)(2,1)S(1)} %get-tuple-element.22), channel_id=1, replica_groups=mesh['row_0'=8,'row_1'=2,'col_0'=8,'col_1'=4] {'row_0','row_1'}, dimensions={0} | all-to-all | bytes 131072 | tf_op jit(solution)/shard_map/all_to_all | solution.py:205
  161.9 2.7 %shard_map.127 = (f32[16,128]{1,0:T(8,128)}, bf16[32,16,128]{2,1,0:T(8,128)(2,1)S(1)}) custom-call(bf16[16,16,128]{2,1,0:T(8,128)(2,1)S(1)} %all_to_all.60.y, f32[16,128]{1,0:T(8,128)S(1)} %get-tuple-element.20.mass, bf16[2048,2048]{1,0:T(8,128)(2,1)S(1)} %get-tuple-element.18.kernel), custom_call_target="tpu_custom_call" | custom-call | tf_op jit(solution)/shard_map/pallas_call | solution.py:194
  164.6 12.8 %all_to_all.61.y = bf16[32,16,128]{2,1,0:T(8,128)(2,1)S(1)} all-to-all(bf16[32,16,128]{2,1,0:T(8,128)(2,1)S(1)} %get-tuple-element.23), channel_id=1, replica_groups=mesh['row_0'=8,'row_1'=2,'col_0'=8,'col_1'=4] {'col_0','col_1'}, dimensions={0} | all-to-all | bytes 262144 | tf_op jit(solution)/shard_map/all_to_all | solution.py:205
  177.5 1.2 shard_map.128
  178.7 11.9 %all_to_all.62.y = bf16[16,16,128]{2,1,0:T(8,128)(2,1)S(1)} all-to-all(bf16[16,16,128]{2,1,0:T(8,128)(2,1)S(1)} %get-tuple-element.24), channel_id=1, replica_groups=mesh['row_0'=8,'row_1'=2,'col_0'=8,'col_1'=4] {'row_0','row_1'}, dimensions={0} | all-to-all | bytes 131072 | tf_op jit(solution)/shard_map/all_to_all | solution.py:205
  190.5 3.8 %shard_map.129 = (f32[16,128]{1,0:T(8,128)}, f32[16,128]{1,0:T(8,128)}, bf16[16,32,128]{2,1,0:T(8,128)(2,1)S(1)}) custom-call(bf16[16,16,128]{2,1,0:T(8,128)(2,1)S(1)} %all_to_all.62.y, f32[16,128]{1,0:T(8,128)S(1)} %get-tuple-element.20.mass, f32[16,128]{1,0:T(8,128)S(1)} %get-tuple-element.25.row_scale, bf16[2048,2048]{1,0:T(8,128)(2,1)S(1)} %get-tuple-element.18.kernel, ...), custom_call_target="tpu_custom_call" | custom-call | tf_op jit(solution)/shard_map/pallas_call | solution.py:194
  194.3 11.7 %all_to_all.63.y = bf16[16,32,128]{2,1,0:T(8,128)(2,1)S(1)} all-to-all(bf16[16,32,128]{2,1,0:T(8,128)(2,1)S(1)} %get-tuple-element.28), channel_id=1, replica_groups=mesh['row_0'=8,'row_1'=2,'col_0'=8,'col_1'=4] {'row_0','row_1'}, dimensions={0} | all-to-all | bytes 262144 | tf_op jit(solution)/shard_map/all_to_all | solution.py:205
  206.1 15.4 %all_to_all.64.y = bf16[32,32,128]{2,1,0:T(8,128)(2,1)S(1)} all-to-all(bf16[32,32,128]{2,1,0:T(8,128)(2,1)S(1)} %shard_map.130), channel_id=1, replica_groups=mesh['row_0'=8,'row_1'=2,'col_0'=8,'col_1'=4] {'col_0','col_1'}, dimensions={0} | all-to-all | bytes 524288 | tf_op jit(solution)/shard_map/all_to_all | solution.py:205
  (23 shorter events, 3.4 us)
Async XLA Ops:
  0.6 96.0 %copy-start.7 = (f32[2048]{0:T(1024)S(1)}, f32[2048]{0:T(1024)}, u32[]{:S(2)}) copy-start(f32[2048]{0:T(1024)} %param.19) | copy-start | bytes 24580
  0.6 96.0 %copy-start.3 = (f32[2048]{0:T(1024)S(1)}, f32[2048]{0:T(1024)}, u32[]{:S(2)}) copy-start(f32[2048]{0:T(1024)} %param.18) | copy-start | bytes 24580
  0.7 96.0 %copy-start.5 = (f32[2048]{0:T(1024)S(1)}, f32[2048]{0:T(1024)}, u32[]{:S(2)}) copy-start(f32[2048]{0:T(1024)} %param.14) | copy-start | bytes 24580
  0.7 96.0 %copy-start.1 = (f32[2048]{0:T(1024)S(1)}, f32[2048]{0:T(1024)}, u32[]{:S(2)}) copy-start(f32[2048]{0:T(1024)} %param.13) | copy-start | bytes 24580
  2.8 35.2 %all-to-all-start = ((bf16[32,2,6144]{2,1,0:T(2,128)(2,1)}), bf16[32,2,6144]{2,1,0:T(2,128)(2,1)S(1)}, u32[]{:S(2)}, u32[]{:S(2)}) async-start(bf16[32,2,6144]{2,1,0:T(2,128)(2,1)} %broadcast_in_dim.2), calls=%async_computation | async-start | bytes 1572864 | tf_op jit(solution)/shard_map/all_to_all | solution.py:205
  38.3 0.7 copy-start
  39.0 0.7 copy-start.2
  39.7 0.7 copy-start.4
  40.4 0.7 copy-start.6

commit v3 on v2

v3 whole, which is shorter than its diff:
```python
import functools
import math

import jax
import jax.numpy as jnp
from jax import lax
from jax.experimental import pallas as pl
from jax.experimental.pallas import tpu as pltpu
from jax.sharding import Mesh
from jax.sharding import PartitionSpec as P

SWEEPS = 3
ROW = ("row_0", "row_1")
COL = ("col_0", "col_1")
F32 = jnp.float32
BF16 = jnp.bfloat16
LANES = 128
CHUNK = 4
PAD = 16

VMEM = pl.BlockSpec(memory_space=pltpu.VMEM)
FIRST = (((0,), (0,)), ((), ()))
LAST = (((1,), (1,)), ((), ()))
PLAIN = (((1,), (0,)), ((), ()))


def dot(a, b, dims):
    return lax.dot_general(a, b, dims, preferred_element_type=F32)


def three_parts(v):
    high = v.astype(BF16).astype(F32)
    rest = v - high
    mid = rest.astype(BF16).astype(F32)
    low = (rest - mid).astype(BF16).astype(F32)
    return high, mid, low


def logit_rows(v, first):
    n = v.shape[1]
    row = lax.broadcasted_iota(jnp.int32, (PAD, n), 0)
    at, ones = (0, 3) if first else (3, 0)
    out = jnp.where((row >= ones) & (row < ones + 3), 1.0, 0.0)
    for index, part in enumerate(three_parts(v)):
        out = jnp.where(row == at + index, jnp.broadcast_to(part, (PAD, n)), out)
    return out.astype(BF16)


def to_lanes(v, flat_ref):
    for s in range(v.shape[0]):
        flat_ref[:, s * LANES : (s + 1) * LANES] = jnp.broadcast_to(v[s : s + 1], (8, LANES))
    return flat_ref[...]


def to_tiles(row, tile_ref):
    for s in range(tile_ref.shape[0]):
        tile_ref[s : s + 1, :] = row[:, s * LANES : (s + 1) * LANES]
    return tile_ref[...]


def send(out_ref, v):
    v = v.astype(out_ref.dtype)
    for p in range(out_ref.shape[0]):
        out_ref[p] = v


def received(ref):
    total = ref[0].astype(F32)
    for p in range(1, ref.shape[0]):
        total = total + ref[p].astype(F32)
    return total


def halves_on_lanes(core, rank):
    half = rank // 2
    lane = lax.broadcasted_iota(jnp.int32, (half, 2 * rank), 1)
    return jnp.where(lane < rank, core[:half], core[half:rank])


def fetch(there, here, sem):
    copies = [pltpu.make_async_copy(t, h, sem.at[k]) for k, (t, h) in enumerate(zip(there, here))]
    for copy in copies:
        copy.start()
    return copies


def pack_kernel(*refs):
    there, (src_out, tgt_out), here, sem = refs[:6], refs[6:8], refs[8:14], refs[14]
    for copy in fetch(there, here, sem):
        copy.wait()
    mine = jnp.concatenate([ref[...] for ref in here[:3]], axis=1)
    for p in range(src_out.shape[0]):
        src_out[p] = mine
    tgt_out[...] = jnp.concatenate([ref[...] for ref in here[3:]], axis=1)


def opening_kernel(
    src, tgt, src_logit_in, tgt_logit_in, src_weight_in, tgt_weight_in, out,
    xs, xt, right, src_logit, tgt_logit, src_weight, tgt_weight, sem,
):
    copies = fetch(
        (src_logit_in, tgt_logit_in, src_weight_in, tgt_weight_in),
        (src_logit, tgt_logit, src_weight, tgt_weight),
        sem,
    )
    rank = src.shape[0]
    n = src_logit.shape[1]
    m = tgt_logit.shape[1]
    xs[:rank] = (src[:, :n].astype(F32) * 0.125).astype(BF16)
    xt[:rank] = tgt[:, :m]
    right[:rank] = tgt[:, 2 * m :]
    right[rank : 2 * rank] = tgt[:, 2 * m :]
    row = lax.broadcasted_iota(jnp.int32, (PAD, m), 0)
    right[2 * rank :] = jnp.where(row == 0, 1.0, 0.0).astype(BF16)
    for copy in copies:
        copy.wait()
    xs[rank:] = logit_rows(src_logit[...], True)
    xt[rank:] = logit_rows(tgt_logit[...], False)
    tile = jnp.exp(dot(xs[...], xt[...], FIRST)).astype(BF16)
    side = dot(tile, right[...], LAST)
    row = lax.broadcasted_iota(jnp.int32, (PAD, n), 0)
    left = jnp.concatenate([src[:, 2 * n :], jnp.where(row == 0, 1.0, 0.0).astype(BF16)], axis=0)
    both = sum(dot(left, part.astype(BF16), PLAIN) for part in three_parts(side))
    core = halves_on_lanes(both[:, : 2 * rank], rank)
    total = both[rank : rank + 1, 2 * rank : 2 * rank + 1]
    src_sum = jnp.sum(src_weight[...], keepdims=True)
    tgt_sum = jnp.sum(tgt_weight[...], keepdims=True)
    half = CHUNK // 2
    lane = lax.broadcasted_iota(jnp.int32, (half, LANES), 1)
    sums = jnp.where(
        lane == 0, total, jnp.where(lane == 1, src_sum, jnp.where(lane == 2, tgt_sum, 0.0))
    )
    for p in range(out.shape[0]):
        out[p, :half] = core[p * half : (p + 1) * half]
        out[p, half:] = sums


def relay_kernel(y, out):
    send(out, received(y))


def tile_kernel(
    mass_scale, row_peers, col_peers,
    z, src, tgt, src_logit_in, tgt_logit_in, src_weight_in, tgt_weight_in,
    kernel, out, row_mass, col_mass,
    xs, xt, tiles, core, src_logit, tgt_logit, src_weight, tgt_weight, sem,
):
    copies = fetch(
        (src_logit_in, tgt_logit_in, src_weight_in, tgt_weight_in),
        (src_logit, tgt_logit, src_weight, tgt_weight),
        sem,
    )
    rank = src.shape[0]
    half = rank // 2
    few = CHUNK // 2
    n = src_logit.shape[1]
    m = tgt_logit.shape[1]
    for p in range(row_peers):
        core[p * few : (p + 1) * few] = z[p, :few]
    sums = z[0, few : few + 1]
    grand_total = sums[:, 0:1]
    mixing = mass_scale * core[...] / grand_total
    parts = jnp.concatenate(three_parts(mixing), axis=0).astype(BF16)
    top = src[:half, n : 2 * n]
    bottom = src[half:, n : 2 * n]
    top = dot(parts, jnp.concatenate([top, top, top], axis=0), FIRST)
    bottom = dot(parts, jnp.concatenate([bottom, bottom, bottom], axis=0), FIRST)
    xs[:rank] = (src[:, :n].astype(F32) * 0.125).astype(BF16)
    xs[rank : 2 * rank] = (2.0 * (top[:rank] + bottom[rank:])).astype(BF16)
    for copy in copies:
        copy.wait()
    row_mass[...] = src_weight[...] / (sums[:, 1:2] / col_peers)
    col_mass[...] = tgt_weight[...] / (sums[:, 2:3] / row_peers)
    xs[2 * rank :] = logit_rows(src_logit[...], True)
    xt[:rank] = tgt[:, :m]
    xt[rank : 2 * rank] = tgt[:, m : 2 * m]
    xt[2 * rank :] = logit_rows(tgt_logit[...] - jnp.log(grand_total), False)
    tile = jnp.exp(dot(xs[...], xt[...], FIRST)).astype(BF16)
    kernel[...] = tile
    totals = dot(jnp.ones((PAD, m), BF16), tile, LAST)
    send(out, to_tiles(totals[0:1], tiles))


def sweep_kernel(over_rows, y, mass, kernel, scale, out, flat, tiles):
    s = mass[...] / received(y)
    scale[...] = s
    weights = to_lanes(s, flat).astype(BF16)
    total = dot(weights, kernel[...], PLAIN if over_rows else LAST)
    send(out, to_tiles(total[0:1], tiles))


def side_kernel(shift, row_scale, kernel, src, row_potential, side, flat):
    rank = src.shape[0]
    n = kernel.shape[0]
    row_potential[...] = jnp.log(row_scale[...]) + shift
    rows = to_lanes(row_scale[...], flat)
    left = src[:, 2 * n :].astype(F32) * rows[0:1]
    parts = jnp.concatenate(three_parts(left), axis=0).astype(BF16)
    total = dot(parts, kernel[...], PLAIN)
    side[...] = total[:rank] + total[rank : 2 * rank] + total[2 * rank :]


def closing_kernel(y, mass, side, tgt, col_potential, out, flat, twice):
    rank, m = side.shape
    col_scale = mass[...] / received(y)
    col_potential[...] = jnp.log(col_scale)
    cols = to_lanes(col_scale, flat)
    scaled = (tgt[:, 2 * m :].astype(F32) * cols[0:1]).astype(BF16)
    twice[:rank] = scaled
    twice[rank:] = scaled
    parts = jnp.concatenate(three_parts(side[...]), axis=0).astype(BF16)
    total = dot(parts, twice[...], LAST)
    send(out, halves_on_lanes(total[:rank] + total[rank : 2 * rank] + total[2 * rank :], rank))


def final_kernel(mass_scale, y, out):
    core = mass_scale * received(y)
    half, rank = core.shape[0], core.shape[1] // 2
    out[:half] = core[:, :rank]
    out[half:] = core[:, rank:]


def call(body, outs, scratch, *args, stay=0, room=8):
    here, there = args[: len(args) - stay], args[len(args) - stay :]
    there = [pltpu.with_memory_space_constraint(a, pltpu.HBM) for a in there]
    return pl.pallas_call(
        body,
        out_shape=[jax.ShapeDtypeStruct(s, d) for s, d in outs],
        in_specs=[VMEM] * (len(args) - stay) + [pl.BlockSpec(memory_space=pltpu.HBM)] * stay,
        out_specs=[VMEM] * len(outs),
        scratch_shapes=[pltpu.VMEM(*x) if isinstance(x, tuple) else x for x in scratch],
        compiler_params=pltpu.CompilerParams(vmem_limit_bytes=room << 20),
    )(*here, *there)


def exchange(value, axis):
    return lax.all_to_all(value, axis, 0, 0, tiled=True)


def body(
    src_embed,
    src_left,
    src_right,
    src_logit,
    src_weight,
    tgt_embed,
    tgt_left,
    tgt_right,
    tgt_logit,
    tgt_weight,
):
    n, m = src_logit.shape[0], tgt_logit.shape[0]
    row_peers, col_peers = lax.axis_size(ROW), lax.axis_size(COL)
    n_all, m_all = n * row_peers, m * col_peers
    rank = src_embed.shape[0] * col_peers
    half = rank // 2
    mass_scale = math.sqrt(n_all * m_all)
    nt, mt = n // LANES, m // LANES

    src, tgt = call(
        pack_kernel,
        [
            ((col_peers, rank // col_peers, 3 * n), BF16),
            ((rank // row_peers, 3 * m), BF16),
        ],
        [
            *[(a.shape, BF16) for a in (src_embed, src_left, src_right)],
            *[(a.shape, BF16) for a in (tgt_embed, tgt_left, tgt_right)],
            pltpu.SemaphoreType.DMA((6,)),
        ],
        src_embed, src_left, src_right, tgt_embed, tgt_left, tgt_right, stay=6,
    )
    src = exchange(src, COL).reshape(rank, 3 * n)
    tgt = lax.all_gather(tgt, ROW, axis=0, tiled=True)
    src_logit, tgt_logit = src_logit.reshape(1, n), tgt_logit.reshape(1, m)
    src_weight, tgt_weight = src_weight.reshape(nt, LANES), tgt_weight.reshape(mt, LANES)

    (part,) = call(
        opening_kernel,
        [((row_peers, CHUNK, LANES), F32)],
        [
            ((rank + PAD, n), BF16),
            ((rank + PAD, m), BF16),
            ((2 * rank + PAD, m), BF16),
            ((1, n), F32),
            ((1, m), F32),
            ((nt, LANES), F32),
            ((mt, LANES), F32),
            pltpu.SemaphoreType.DMA((4,)),
        ],
        src, tgt, src_logit, tgt_logit, src_weight, tgt_weight, stay=4, room=32,
    )
    (part,) = call(relay_kernel, [((col_peers, CHUNK, LANES), F32)], [], exchange(part, ROW))
    (part,) = call(relay_kernel, [((row_peers, CHUNK, LANES), F32)], [], exchange(part, COL))
    kernel, part, row_mass, col_mass = call(
        functools.partial(tile_kernel, mass_scale, row_peers, col_peers),
        [
            ((n, m), BF16),
            ((col_peers, nt, LANES), BF16),
            ((nt, LANES), F32),
            ((mt, LANES), F32),
        ],
        [
            ((2 * rank + PAD, n), BF16),
            ((2 * rank + PAD, m), BF16),
            ((nt, LANES), F32),
            ((half, LANES), F32),
            ((1, n), F32),
            ((1, m), F32),
            ((nt, LANES), F32),
            ((mt, LANES), F32),
            pltpu.SemaphoreType.DMA((4,)),
        ],
        exchange(part, ROW), src, tgt, src_logit, tgt_logit, src_weight, tgt_weight,
        stay=4, room=32,
    )
    for sweep in range(SWEEPS):
        row_scale, part = call(
            functools.partial(sweep_kernel, True),
            [((nt, LANES), F32), ((row_peers, mt, LANES), BF16)],
            [((8, n), F32), ((mt, LANES), F32)],
            exchange(part, COL), row_mass, kernel,
        )
        part = exchange(part, ROW)
        if sweep + 1 < SWEEPS:
            _, part = call(
                functools.partial(sweep_kernel, False),
                [((mt, LANES), F32), ((col_peers, nt, LANES), BF16)],
                [((8, m), F32), ((nt, LANES), F32)],
                part, col_mass, kernel,
            )
    row_potential, side = call(
        functools.partial(side_kernel, math.log(n_all) + math.log(m_all)),
        [((nt, LANES), F32), ((rank, m), F32)],
        [((8, n), F32)],
        row_scale, kernel, src,
    )
    col_potential, part = call(
        closing_kernel,
        [((mt, LANES), F32), ((row_peers, half, LANES), BF16)],
        [((8, m), F32), ((2 * rank, m), BF16)],
        part, col_mass, side, tgt,
    )
    (part,) = call(relay_kernel, [((col_peers, half, LANES), BF16)], [], exchange(part, ROW))
    (new_core,) = call(
        functools.partial(final_kernel, mass_scale), [((rank, rank), F32)], [], exchange(part, COL)
    )
    return (row_potential.reshape(n), col_potential.reshape(m), new_core)


def solution(mesh):
    torus = Mesh(mesh.devices.reshape(8, 2, 8, 4), ("row_0", "row_1", "col_0", "col_1"))
    placed = (
        P(COL, ROW),
        P(COL, ROW),
        P(COL, ROW),
        P(ROW),
        P(ROW),
        P(ROW, COL),
        P(ROW, COL),
        P(ROW, COL),
        P(COL),
        P(COL),
    )
    return jax.shard_map(
        body, mesh=torus, in_specs=placed, out_specs=(P(ROW), P(COL), P()), check_vma=False
    )
```

time: 223 us -> 209 us (0.937)
  blocking collectives: 170 us -> 154 us
  starting transfers between devices: 13.7 us -> 18.7 us
  waiting for transfers between devices: 0.01 us -> 2.52 us
    all_to_all x10, blocking collectives: 150 us -> 133 us  [exchange(): return lax.all_to_all(value, axis, 0, 0, tiled=True)]
    all_to_all x1 -> x2, starting transfers between devices: 13.7 us -> 18.7 us  [exchange(): return lax.all_to_all(value, axis, 0, 0, tiled=True)]
    all_to_all x1 -> x2, waiting for transfers between devices: 0.01 us -> 2.52 us  [exchange(): return lax.all_to_all(value, axis, 0, 0, tiled=True)]
    pallas_call x11 -> x14, Pallas kernels: 30.5 us -> 28.5 us  [call(): pl.pallas_call(body, out_shape=[jax.ShapeDtypeStruct(s, d) for s, d in ou...]
  transfers between devices with their start and end apart: 1 -> 2, of which waited for: 0 -> 2; matrix products, arithmetic and copies ran while one was open for 0% -> 0% of each run, Pallas kernels for 0% -> 1%
where the time goes in v3:
time: 209 us; the launch traced here: 208 us
  blocking collectives  154 us (74%)
  Pallas kernels  28.5 us (14%)
  starting transfers between devices  18.7 us (9%)
  local copies, waits for them, and re-layouts  3.85 us (2%)
  waiting for transfers between devices  2.52 us (1%)
    all_to_all x10, blocking collectives, exchange(): return lax.all_to_all(value, axis, 0, 0, tiled=True)  133 us
    pallas_call x14, Pallas kernels, call(): pl.pallas_call(body, out_shape=[jax.ShapeDtypeStruct(s, d) for s, d in ou...  28.5 us
    all_gather x1, blocking collectives, body(): tgt = lax.all_gather(tgt, ROW, axis=0, tiled=True)  20.5 us
    all_to_all x2, starting transfers between devices, exchange(): return lax.all_to_all(value, axis, 0, 0, tiled=True)  18.7 us
  transfers between devices with their start and end apart: 2, of which 2 were waited for; matrix products, arithmetic and copies ran while one was open for 0% of the time, Pallas kernels for 1%

profile of v3, /device:TPU:1, one launch (start us, length us, event | category | flops | bytes accessed | tf_op | source)
XLA Modules:
  0.0 208.0 jit_solution(17937326515980672179)
XLA Ops:
  0.6 1.8 shard_map.121
  2.5 13.7 %all-to-all-start = ((bf16[32,2,6144]{2,1,0:T(2,128)(2,1)}), bf16[32,2,6144]{2,1,0:T(2,128)(2,1)S(1)}, u32[]{:S(2)}, u32[]{:S(2)}) async-start(bf16[32,2,6144]{2,1,0:T(2,128)(2,1)} %get-tuple-element.19), calls=%async_computation | async-start | bytes 1572864 | tf_op jit(solution)/shard_map/all_to_all | solution.py:237
  16.2 20.5 %all-gather = bf16[16,4,6144]{2,1,0:T(4,128)(2,1)S(1)} all-gather(bf16[1,4,6144]{2,1,0:T(4,128)(2,1)S(1)} %bitcast.7), channel_id=1, replica_groups=mesh['row_0'=8,'row_1'=2,'col_0'=8,'col_1'=4] {'row_0','row_1'}, dimensions={0}, use_global_device_ids=true | all-gather | bytes 835584 | tf_op jit(solution)/shard_map/all_gather | solution.py:274
  37.6 6.6 %shard_map.122 = f32[16,4,128]{2,1,0:T(4,128)S(1)} custom-call(bf16[64,6144]{1,0:T(8,128)(2,1)S(1)} %reshape.27.src, bf16[64,6144]{1,0:T(8,128)(2,1)S(1)} %reshape.35.tgt, f32[1,2048]{1,0:T(1,128)} %bitcast.8, f32[1,2048]{1,0:T(1,128)} %bitcast.10, f32[16,128]{1,0:T(8,128)} %bitcast.12, f32[16,128]{1,0:T(8,128)} %bitcast.14), custom_call_target="tpu_custom_call" | custom-call | tf_op jit(solution)/shard_map/pallas_call | solution.py:226
  44.1 17.1 %all_to_all.60.y = f32[16,4,128]{2,1,0:T(4,128)S(1)} all-to-all(f32[16,4,128]{2,1,0:T(4,128)S(1)} %shard_map.122), channel_id=1, replica_groups=mesh['row_0'=8,'row_1'=2,'col_0'=8,'col_1'=4] {'row_0','row_1'}, dimensions={0} | all-to-all | bytes 65536 | tf_op jit(solution)/shard_map/all_to_all | solution.py:237
  61.2 13.5 %all_to_all.61.y = f32[32,4,128]{2,1,0:T(4,128)S(1)} all-to-all(f32[32,4,128]{2,1,0:T(4,128)S(1)} %shard_map.123), channel_id=1, replica_groups=mesh['row_0'=8,'row_1'=2,'col_0'=8,'col_1'=4] {'col_0','col_1'}, dimensions={0} | all-to-all | bytes 131072 | tf_op jit(solution)/shard_map/all_to_all | solution.py:237
  74.7 11.7 %all_to_all.62.z = f32[16,4,128]{2,1,0:T(4,128)S(1)} all-to-all(f32[16,4,128]{2,1,0:T(4,128)S(1)} %shard_map.124), channel_id=1, replica_groups=mesh['row_0'=8,'row_1'=2,'col_0'=8,'col_1'=4] {'row_0','row_1'}, dimensions={0} | all-to-all | bytes 65536 | tf_op jit(solution)/shard_map/all_to_all | solution.py:237
  86.4 5.4 %shard_map.125 = (bf16[2048,2048]{1,0:T(8,128)(2,1)S(1)}, bf16[32,16,128]{2,1,0:T(8,128)(2,1)S(1)}, f32[16,128]{1,0:T(8,128)S(1)}, f32[16,128]{1,0:T(8,128)S(1)}) custom-call(f32[16,4,128]{2,1,0:T(4,128)S(1)} %all_to_all.62.z, bf16[64,6144]{1,0:T(8,128)(2,1)S(1)} %reshape.27.src, bf16[64,6144]{1,0:T(8,128)(2,1)S(1)} %reshape.35.tgt, f32[1,2048]{1,0:T(1,128)} %bitcast.9, ...), custom_call_target="tpu_custom_call" | custom-call | tf_op jit(solution)/shard_map/pallas_call | solution.py:226
  91.9 12.4 %all_to_all.63.y = bf16[32,16,128]{2,1,0:T(8,128)(2,1)S(1)} all-to-all(bf16[32,16,128]{2,1,0:T(8,128)(2,1)S(1)} %get-tuple-element.21), channel_id=1, replica_groups=mesh['row_0'=8,'row_1'=2,'col_0'=8,'col_1'=4] {'col_0','col_1'}, dimensions={0} | all-to-all | bytes 262144 | tf_op jit(solution)/shard_map/all_to_all | solution.py:237
  104.2 1.7 shard_map.126
  105.9 12.3 %all_to_all.64.y = bf16[16,16,128]{2,1,0:T(8,128)(2,1)S(1)} all-to-all(bf16[16,16,128]{2,1,0:T(8,128)(2,1)S(1)} %get-tuple-element.24), channel_id=1, replica_groups=mesh['row_0'=8,'row_1'=2,'col_0'=8,'col_1'=4] {'row_0','row_1'}, dimensions={0} | all-to-all | bytes 131072 | tf_op jit(solution)/shard_map/all_to_all | solution.py:237
  118.2 2.7 %shard_map.127 = (f32[16,128]{1,0:T(8,128)}, bf16[32,16,128]{2,1,0:T(8,128)(2,1)S(1)}) custom-call(bf16[16,16,128]{2,1,0:T(8,128)(2,1)S(1)} %all_to_all.64.y, f32[16,128]{1,0:T(8,128)S(1)} %get-tuple-element.25.mass, bf16[2048,2048]{1,0:T(8,128)(2,1)S(1)} %get-tuple-element.23.kernel), custom_call_target="tpu_custom_call" | custom-call | tf_op jit(solution)/shard_map/pallas_call | solution.py:226
  121.0 12.8 %all_to_all.65.y = bf16[32,16,128]{2,1,0:T(8,128)(2,1)S(1)} all-to-all(bf16[32,16,128]{2,1,0:T(8,128)(2,1)S(1)} %get-tuple-element.26), channel_id=1, replica_groups=mesh['row_0'=8,'row_1'=2,'col_0'=8,'col_1'=4] {'col_0','col_1'}, dimensions={0} | all-to-all | bytes 262144 | tf_op jit(solution)/shard_map/all_to_all | solution.py:237
  133.7 1.7 shard_map.128
  135.4 11.9 %all_to_all.66.y = bf16[16,16,128]{2,1,0:T(8,128)(2,1)S(1)} all-to-all(bf16[16,16,128]{2,1,0:T(8,128)(2,1)S(1)} %get-tuple-element.27), channel_id=1, replica_groups=mesh['row_0'=8,'row_1'=2,'col_0'=8,'col_1'=4] {'row_0','row_1'}, dimensions={0} | all-to-all | bytes 131072 | tf_op jit(solution)/shard_map/all_to_all | solution.py:237
  147.3 2.7 %shard_map.129 = (f32[16,128]{1,0:T(8,128)}, bf16[32,16,128]{2,1,0:T(8,128)(2,1)S(1)}) custom-call(bf16[16,16,128]{2,1,0:T(8,128)(2,1)S(1)} %all_to_all.66.y, f32[16,128]{1,0:T(8,128)S(1)} %get-tuple-element.25.mass, bf16[2048,2048]{1,0:T(8,128)(2,1)S(1)} %get-tuple-element.23.kernel), custom_call_target="tpu_custom_call" | custom-call | tf_op jit(solution)/shard_map/pallas_call | solution.py:226
  150.0 12.8 %all_to_all.67.y = bf16[32,16,128]{2,1,0:T(8,128)(2,1)S(1)} all-to-all(bf16[32,16,128]{2,1,0:T(8,128)(2,1)S(1)} %get-tuple-element.28), channel_id=1, replica_groups=mesh['row_0'=8,'row_1'=2,'col_0'=8,'col_1'=4] {'col_0','col_1'}, dimensions={0} | all-to-all | bytes 262144 | tf_op jit(solution)/shard_map/all_to_all | solution.py:237
  162.8 1.9 shard_map.130
  164.7 5.0 %all-to-all-start.9 = ((bf16[16,16,128]{2,1,0:T(8,128)(2,1)}), bf16[16,16,128]{2,1,0:T(8,128)(2,1)S(1)}, u32[]{:S(2)}, u32[]{:S(2)}) async-start(bf16[16,16,128]{2,1,0:T(8,128)(2,1)} %get-tuple-element.31), calls=%async_computation.9 | async-start | bytes 131072 | tf_op jit(solution)/shard_map/all_to_all | solution.py:237
  169.7 3.4 %copy-done.1 = bf16[2048,2048]{1,0:T(8,128)(2,1)S(1)} copy-done((bf16[2048,2048]{1,0:T(8,128)(2,1)S(1)}, bf16[2048,2048]{1,0:T(8,128)(2,1)}, u32[]{:S(2)}) %copy-start.1) | copy-done | bytes 8388632
  173.0 2.3 %shard_map.131 = (f32[16,128]{1,0:T(8,128)}, f32[64,2048]{1,0:T(8,128)S(1)}) custom-call(f32[16,128]{1,0:T(8,128)S(1)} %get-tuple-element.29.row_scale, bf16[2048,2048]{1,0:T(8,128)(2,1)S(1)} %copy-done.1, bf16[64,6144]{1,0:T(8,128)(2,1)S(1)} %reshape.27.src), custom_call_target="tpu_custom_call" | custom-call | tf_op jit(solution)/shard_map/pallas_call | solution.py:226
  175.3 2.2 %all-to-all-done.9.y = bf16[16,16,128]{2,1,0:T(8,128)(2,1)S(1)} async-done(((bf16[16,16,128]{2,1,0:T(8,128)(2,1)}), bf16[16,16,128]{2,1,0:T(8,128)(2,1)S(1)}, u32[]{:S(2)}, u32[]{:S(2)}) %all-to-all-start.9) | async-done | bytes 65568 | tf_op jit(solution)/shard_map/all_to_all | solution.py:237
  178.4 13.8 %all_to_all.68.y = bf16[16,32,128]{2,1,0:T(8,128)(2,1)S(1)} all-to-all(bf16[16,32,128]{2,1,0:T(8,128)(2,1)S(1)} %get-tuple-element.34), channel_id=1, replica_groups=mesh['row_0'=8,'row_1'=2,'col_0'=8,'col_1'=4] {'row_0','row_1'}, dimensions={0} | all-to-all | bytes 262144 | tf_op jit(solution)/shard_map/all_to_all | solution.py:237
  192.2 15.1 %all_to_all.69.y = bf16[32,32,128]{2,1,0:T(8,128)(2,1)S(1)} all-to-all(bf16[32,32,128]{2,1,0:T(8,128)(2,1)S(1)} %shard_map.133), channel_id=1, replica_groups=mesh['row_0'=8,'row_1'=2,'col_0'=8,'col_1'=4] {'col_0','col_1'}, dimensions={0} | all-to-all | bytes 524288 | tf_op jit(solution)/shard_map/all_to_all | solution.py:237
  (11 shorter events, 2.5 us)
Async XLA Ops:
  2.5 34.8 %all-to-all-start = ((bf16[32,2,6144]{2,1,0:T(2,128)(2,1)}), bf16[32,2,6144]{2,1,0:T(2,128)(2,1)S(1)}, u32[]{:S(2)}, u32[]{:S(2)}) async-start(bf16[32,2,6144]{2,1,0:T(2,128)(2,1)} %get-tuple-element.19), calls=%async_computation | async-start | bytes 1572864 | tf_op jit(solution)/shard_map/all_to_all | solution.py:237
  91.9 71.0 %copy-start = (bf16[2048,2048]{1,0:T(8,128)(2,1)}, bf16[2048,2048]{1,0:T(8,128)(2,1)S(1)}, u32[]{:S(2)}) copy-start(bf16[2048,2048]{1,0:T(8,128)(2,1)S(1)} %get-tuple-element.23.kernel) | copy-start | bytes 25165828
  164.7 12.8 %all-to-all-start.9 = ((bf16[16,16,128]{2,1,0:T(8,128)(2,1)}), bf16[16,16,128]{2,1,0:T(8,128)(2,1)S(1)}, u32[]{:S(2)}, u32[]{:S(2)}) async-start(bf16[16,16,128]{2,1,0:T(8,128)(2,1)} %get-tuple-element.31), calls=%async_computation.9 | async-start | bytes 131072 | tf_op jit(solution)/shard_map/all_to_all | solution.py:237
  169.6 3.4 %copy-start.1 = (bf16[2048,2048]{1,0:T(8,128)(2,1)S(1)}, bf16[2048,2048]{1,0:T(8,128)(2,1)}, u32[]{:S(2)}) copy-start(bf16[2048,2048]{1,0:T(8,128)(2,1)} %copy-done) | copy-start | bytes 25165828

commit v4 on v3

--- a/solution.py
+++ b/solution.py
@@ -10,15 +10,16 @@
 from jax.sharding import PartitionSpec as P
 
 SWEEPS = 3
-ROW = ("row_0", "row_1")
+ROW = ("row_0", "row_1", "core")
+NEAR = ("row_1", "core")
 COL = ("col_0", "col_1")
 F32 = jnp.float32
 BF16 = jnp.bfloat16
 LANES = 128
-CHUNK = 4
 PAD = 16
 
 VMEM = pl.BlockSpec(memory_space=pltpu.VMEM)
+HBM = pl.BlockSpec(memory_space=pltpu.HBM)
 FIRST = (((0,), (0,)), ((), ()))
 LAST = (((1,), (1,)), ((), ()))
 PLAIN = (((1,), (0,)), ((), ()))
@@ -34,6 +35,12 @@
     mid = rest.astype(BF16).astype(F32)
     low = (rest - mid).astype(BF16).astype(F32)
     return high, mid, low
+
+
+def in_parts(a, b):
+    rows = a.shape[0]
+    total = dot(jnp.concatenate(three_parts(a), axis=0).astype(BF16), b, LAST)
+    return total[:rows] + total[rows : 2 * rows] + total[2 * rows :]
 
 
 def logit_rows(v, first):
@@ -58,6 +65,15 @@
     return tile_ref[...]
 
 
+def over_lanes(v):
+    width = v.shape[1]
+    total = v[:, :LANES]
+    for s in range(1, width // LANES):
+        total = total + v[:, s * LANES : (s + 1) * LANES]
+    ones = jnp.ones((PAD, LANES), BF16)
+    return sum(dot(ones, part.astype(BF16), LAST)[0:1] for part in three_parts(total))
+
+
 def send(out_ref, v):
     v = v.astype(out_ref.dtype)
     for p in range(out_ref.shape[0]):
@@ -96,7 +112,7 @@
 
 def opening_kernel(
     src, tgt, src_logit_in, tgt_logit_in, src_weight_in, tgt_weight_in, out,
-    xs, xt, right, src_logit, tgt_logit, src_weight, tgt_weight, sem,
+    xs, xt, right, src_logit, tgt_logit, src_weight, tgt_weight, flat, sem,
 ):
     copies = fetch(
         (src_logit_in, tgt_logit_in, src_weight_in, tgt_weight_in),
@@ -117,22 +133,25 @@
     xs[rank:] = logit_rows(src_logit[...], True)
     xt[rank:] = logit_rows(tgt_logit[...], False)
     tile = jnp.exp(dot(xs[...], xt[...], FIRST)).astype(BF16)
-    side = dot(tile, right[...], LAST)
     row = lax.broadcasted_iota(jnp.int32, (PAD, n), 0)
     left = jnp.concatenate([src[:, 2 * n :], jnp.where(row == 0, 1.0, 0.0).astype(BF16)], axis=0)
-    both = sum(dot(left, part.astype(BF16), PLAIN) for part in three_parts(side))
+    both = in_parts(dot(left, tile, PLAIN), right[...])
     core = halves_on_lanes(both[:, : 2 * rank], rank)
     total = both[rank : rank + 1, 2 * rank : 2 * rank + 1]
     src_sum = jnp.sum(src_weight[...], keepdims=True)
     tgt_sum = jnp.sum(tgt_weight[...], keepdims=True)
-    half = CHUNK // 2
-    lane = lax.broadcasted_iota(jnp.int32, (half, LANES), 1)
+    lane = lax.broadcasted_iota(jnp.int32, (1, LANES), 1)
     sums = jnp.where(
         lane == 0, total, jnp.where(lane == 1, src_sum, jnp.where(lane == 2, tgt_sum, 0.0))
     )
+    parts, _, width = flat.shape
+    for q in range(parts):
+        for s in range(width // LANES - 1):
+            k = q * (width // LANES - 1) + s
+            flat[q, :, s * LANES : (s + 1) * LANES] = core[k : k + 1]
+        flat[q, :, width - LANES :] = sums
     for p in range(out.shape[0]):
-        out[p, :half] = core[p * half : (p + 1) * half]
-        out[p, half:] = sums
+        out[p] = flat[p % parts]
 
 
 def relay_kernel(y, out):
@@ -142,7 +161,7 @@
 def tile_kernel(
     mass_scale, row_peers, col_peers,
     z, src, tgt, src_logit_in, tgt_logit_in, src_weight_in, tgt_weight_in,
-    kernel, out, row_mass, col_mass,
+    kernel, flipped, out, row_mass, col_mass,
     xs, xt, tiles, core, src_logit, tgt_logit, src_weight, tgt_weight, sem,
 ):
     copies = fetch(
@@ -152,12 +171,14 @@
     )
     rank = src.shape[0]
     half = rank // 2
-    few = CHUNK // 2
     n = src_logit.shape[1]
     m = tgt_logit.shape[1]
-    for p in range(row_peers):
-        core[p * few : (p + 1) * few] = z[p, :few]
-    sums = z[0, few : few + 1]
+    parts, _, width = z.shape
+    for q in range(parts):
+        for s in range(width // LANES - 1):
+            k = q * (width // LANES - 1) + s
+            core[k : k + 1] = z[q, :, s * LANES : (s + 1) * LANES]
+    sums = z[0, :, width - LANES :]
     grand_total = sums[:, 0:1]
     mixing = mass_scale * core[...] / grand_total
     parts = jnp.concatenate(three_parts(mixing), axis=0).astype(BF16)
@@ -177,16 +198,17 @@
     xt[2 * rank :] = logit_rows(tgt_logit[...] - jnp.log(grand_total), False)
     tile = jnp.exp(dot(xs[...], xt[...], FIRST)).astype(BF16)
     kernel[...] = tile
-    totals = dot(jnp.ones((PAD, m), BF16), tile, LAST)
-    send(out, to_tiles(totals[0:1], tiles))
-
-
-def sweep_kernel(over_rows, y, mass, kernel, scale, out, flat, tiles):
+    flipped[...] = tile.T
+    send(out, to_tiles(over_lanes(tile.astype(F32)), tiles))
+
+
+def sweep_kernel(y, mass, kernel, out, *rest):
+    *scale, flat, tiles = rest
     s = mass[...] / received(y)
-    scale[...] = s
+    for ref in scale:
+        ref[...] = s
     weights = to_lanes(s, flat).astype(BF16)
-    total = dot(weights, kernel[...], PLAIN if over_rows else LAST)
-    send(out, to_tiles(total[0:1], tiles))
+    send(out, to_tiles(dot(weights, kernel[...], PLAIN)[0:1], tiles))
 
 
 def side_kernel(shift, row_scale, kernel, src, row_potential, side, flat):
@@ -200,17 +222,17 @@
     side[...] = total[:rank] + total[rank : 2 * rank] + total[2 * rank :]
 
 
-def closing_kernel(y, mass, side, tgt, col_potential, out, flat, twice):
+def closing_kernel(y, mass, side, tgt, col_potential, out, flat, twice, potential, sem):
     rank, m = side.shape
     col_scale = mass[...] / received(y)
-    col_potential[...] = jnp.log(col_scale)
+    potential[...] = jnp.log(col_scale)
+    (copy,) = fetch([potential], [col_potential], sem)
     cols = to_lanes(col_scale, flat)
     scaled = (tgt[:, 2 * m :].astype(F32) * cols[0:1]).astype(BF16)
     twice[:rank] = scaled
     twice[rank:] = scaled
-    parts = jnp.concatenate(three_parts(side[...]), axis=0).astype(BF16)
-    total = dot(parts, twice[...], LAST)
-    send(out, halves_on_lanes(total[:rank] + total[rank : 2 * rank] + total[2 * rank :], rank))
+    send(out, halves_on_lanes(in_parts(side[...], twice[...]), rank))
+    copy.wait()
 
 
 def final_kernel(mass_scale, y, out):
@@ -220,14 +242,14 @@
     out[half:] = core[:, rank:]
 
 
-def call(body, outs, scratch, *args, stay=0, room=8):
+def call(body, outs, scratch, *args, stay=0, out_stay=0, room=8):
     here, there = args[: len(args) - stay], args[len(args) - stay :]
     there = [pltpu.with_memory_space_constraint(a, pltpu.HBM) for a in there]
     return pl.pallas_call(
         body,
         out_shape=[jax.ShapeDtypeStruct(s, d) for s, d in outs],
-        in_specs=[VMEM] * (len(args) - stay) + [pl.BlockSpec(memory_space=pltpu.HBM)] * stay,
-        out_specs=[VMEM] * len(outs),
+        in_specs=[VMEM] * (len(args) - stay) + [HBM] * stay,
+        out_specs=[HBM] * out_stay + [VMEM] * (len(outs) - out_stay),
         scratch_shapes=[pltpu.VMEM(*x) if isinstance(x, tuple) else x for x in scratch],
         compiler_params=pltpu.CompilerParams(vmem_limit_bytes=room << 20),
     )(*here, *there)
@@ -275,9 +297,11 @@
     src_logit, tgt_logit = src_logit.reshape(1, n), tgt_logit.reshape(1, m)
     src_weight, tgt_weight = src_weight.reshape(nt, LANES), tgt_weight.reshape(mt, LANES)
 
+    near = lax.axis_size(NEAR)
+    width = half * LANES // near + LANES
     (part,) = call(
         opening_kernel,
-        [((row_peers, CHUNK, LANES), F32)],
+        [((row_peers, 1, width), F32)],
         [
             ((rank + PAD, n), BF16),
             ((rank + PAD, m), BF16),
@@ -286,16 +310,18 @@
             ((1, m), F32),
             ((nt, LANES), F32),
             ((mt, LANES), F32),
+            ((near, 1, width), F32),
             pltpu.SemaphoreType.DMA((4,)),
         ],
         src, tgt, src_logit, tgt_logit, src_weight, tgt_weight, stay=4, room=32,
     )
-    (part,) = call(relay_kernel, [((col_peers, CHUNK, LANES), F32)], [], exchange(part, ROW))
-    (part,) = call(relay_kernel, [((row_peers, CHUNK, LANES), F32)], [], exchange(part, COL))
-    kernel, part, row_mass, col_mass = call(
+    (part,) = call(relay_kernel, [((col_peers, 1, width), F32)], [], exchange(part, ROW))
+    (part,) = call(relay_kernel, [((near, 1, width), F32)], [], exchange(part, COL))
+    kernel, flipped, part, row_mass, col_mass = call(
         functools.partial(tile_kernel, mass_scale, row_peers, col_peers),
         [
             ((n, m), BF16),
+            ((m, n), BF16),
             ((col_peers, nt, LANES), BF16),
             ((nt, LANES), F32),
             ((mt, LANES), F32),
@@ -311,24 +337,26 @@
             ((mt, LANES), F32),
             pltpu.SemaphoreType.DMA((4,)),
         ],
-        exchange(part, ROW), src, tgt, src_logit, tgt_logit, src_weight, tgt_weight,
+        exchange(part, NEAR), src, tgt, src_logit, tgt_logit, src_weight, tgt_weight,
         stay=4, room=32,
     )
     for sweep in range(SWEEPS):
-        row_scale, part = call(
-            functools.partial(sweep_kernel, True),
-            [((nt, LANES), F32), ((row_peers, mt, LANES), BF16)],
+        last = sweep + 1 == SWEEPS
+        part, *row_scale = call(
+            sweep_kernel,
+            [((row_peers, mt, LANES), BF16), ((nt, LANES), F32)][: 1 + last],
             [((8, n), F32), ((mt, LANES), F32)],
             exchange(part, COL), row_mass, kernel,
         )
         part = exchange(part, ROW)
-        if sweep + 1 < SWEEPS:
-            _, part = call(
-                functools.partial(sweep_kernel, False),
-                [((mt, LANES), F32), ((col_peers, nt, LANES), BF16)],
+        if not last:
+            (part,) = call(
+                sweep_kernel,
+                [((col_peers, nt, LANES), BF16)],
                 [((8, m), F32), ((nt, LANES), F32)],
-                part, col_mass, kernel,
+                part, col_mass, flipped,
             )
+    (row_scale,) = row_scale
     row_potential, side = call(
         functools.partial(side_kernel, math.log(n_all) + math.log(m_all)),
         [((nt, LANES), F32), ((rank, m), F32)],
@@ -338,8 +366,8 @@
     col_potential, part = call(
         closing_kernel,
         [((mt, LANES), F32), ((row_peers, half, LANES), BF16)],
-        [((8, m), F32), ((2 * rank, m), BF16)],
-        part, col_mass, side, tgt,
+        [((8, m), F32), ((2 * rank, m), BF16), ((mt, LANES), F32), pltpu.SemaphoreType.DMA((1,))],
+        part, col_mass, side, tgt, out_stay=1,
     )
     (part,) = call(relay_kernel, [((col_peers, half, LANES), BF16)], [], exchange(part, ROW))
     (new_core,) = call(
@@ -349,7 +377,7 @@
 
 
 def solution(mesh):
-    torus = Mesh(mesh.devices.reshape(8, 2, 8, 4), ("row_0", "row_1", "col_0", "col_1"))
+    torus = Mesh(mesh.devices.reshape(4, 2, 2, 8, 4), ("row_0", "row_1", "core", "col_0", "col_1"))
     placed = (
         P(COL, ROW),
         P(COL, ROW),

time: 209 us -> 201 us (0.962)
  Pallas kernels: 28.5 us -> 22.7 us
  blocking collectives: 154 us -> 151 us
    pallas_call x14, Pallas kernels: 28.5 us -> 22.7 us  [call(): pl.pallas_call(body, out_shape=[jax.ShapeDtypeStruct(s, d) for s, d in ou...]
    all_to_all x10, blocking collectives: 133 us -> 131 us  [exchange(): return lax.all_to_all(value, axis, 0, 0, tiled=True)]
where the time goes in v4:
time: 201 us; the launch traced here: 200 us
  blocking collectives  151 us (75%)
  Pallas kernels  22.7 us (11%)
  starting transfers between devices  18.6 us (9%)
  local copies, waits for them, and re-layouts  3.85 us (2%)
  waiting for transfers between devices  2.52 us (1%)
    all_to_all x10, blocking collectives, exchange(): return lax.all_to_all(value, axis, 0, 0, tiled=True)  131 us
    pallas_call x14, Pallas kernels, call(): pl.pallas_call(body, out_shape=[jax.ShapeDtypeStruct(s, d) for s, d in ou...  22.7 us
    all_gather x1, blocking collectives, body(): tgt = lax.all_gather(tgt, ROW, axis=0, tiled=True)  20.5 us
    all_to_all x2, starting transfers between devices, exchange(): return lax.all_to_all(value, axis, 0, 0, tiled=True)  18.6 us
  transfers between devices with their start and end apart: 2, of which 2 were waited for; matrix products, arithmetic and copies ran while one was open for 0% of the time, Pallas kernels for 1%

profile of v4, /device:TPU:1, one launch (start us, length us, event | category | flops | bytes accessed | tf_op | source)
XLA Modules:
  0.0 199.8 jit_solution(5845537435258965264)
XLA Ops:
  0.6 1.8 shard_map.121
  2.4 13.7 %all-to-all-start = ((bf16[32,2,6144]{2,1,0:T(2,128)(2,1)}), bf16[32,2,6144]{2,1,0:T(2,128)(2,1)S(1)}, u32[]{:S(2)}, u32[]{:S(2)}) async-start(bf16[32,2,6144]{2,1,0:T(2,128)(2,1)} %get-tuple-element.16), calls=%async_computation | async-start | bytes 1572864 | tf_op jit(solution)/shard_map/all_to_all | solution.py:259
  16.2 20.5 %all-gather = bf16[16,4,6144]{2,1,0:T(4,128)(2,1)S(1)} all-gather(bf16[1,4,6144]{2,1,0:T(4,128)(2,1)S(1)} %bitcast.7), channel_id=1, replica_groups=mesh['row_0'=4,'row_1'=2,'core'=2,'col_0'=8,'col_1'=4] {'row_0','row_1',..., dimensions={0}, use_global_device_ids=true | all-gather | bytes 835584 | tf_op jit(solution)/shard_map/all_gather | solution.py:296
  37.5 5.0 %shard_map.122 = f32[16,1,1152]{2,1,0:T(1,128)S(1)} custom-call(bf16[64,6144]{1,0:T(8,128)(2,1)S(1)} %reshape.27.src, bf16[64,6144]{1,0:T(8,128)(2,1)S(1)} %reshape.35.tgt, f32[1,2048]{1,0:T(1,128)} %bitcast.8, f32[1,2048]{1,0:T(1,128)} %bitcast.10, f32[16,128]{1,0:T(8,128)} %bitcast.12, f32[16,128]{1,0:T(8,128)} %bitcast.14), custom_call_target="tpu_custom_call" | custom-call | tf_op jit(solution)/shard_map/pallas_call | solution.py:248
  42.5 17.6 %all_to_all.60.y = f32[16,1,1152]{2,1,0:T(1,128)S(1)} all-to-all(f32[16,1,1152]{2,1,0:T(1,128)S(1)} %shard_map.122), channel_id=1, replica_groups=mesh['row_0'=4,'row_1'=2,'core'=2,'col_0'=8,'col_1'=4] {'row_0','row_1',..., dimensions={0} | all-to-all | bytes 147456 | tf_op jit(solution)/shard_map/all_to_all | solution.py:259
  60.2 14.7 %all_to_all.61.y = f32[32,1,1152]{2,1,0:T(1,128)S(1)} all-to-all(f32[32,1,1152]{2,1,0:T(1,128)S(1)} %shard_map.123), channel_id=1, replica_groups=mesh['row_0'=4,'row_1'=2,'core'=2,'col_0'=8,'col_1'=4] {'col_0','col_1'}, dimensions={0} | all-to-all | bytes 294912 | tf_op jit(solution)/shard_map/all_to_all | solution.py:259
  74.9 7.0 %all_to_all.62.z = f32[4,1,1152]{2,1,0:T(1,128)S(1)} all-to-all(f32[4,1,1152]{2,1,0:T(1,128)S(1)} %shard_map.124), channel_id=1, replica_groups=mesh['row_0'=4,'row_1'=2,'core'=2,'col_0'=8,'col_1'=4] {'row_1','core'}, dimensions={0} | all-to-all | bytes 36864 | tf_op jit(solution)/shard_map/all_to_all | solution.py:259
  82.0 5.3 %shard_map.125 = (bf16[2048,2048]{1,0:T(8,128)(2,1)S(1)}, bf16[2048,2048]{1,0:T(8,128)(2,1)S(1)}, bf16[32,16,128]{2,1,0:T(8,128)(2,1)S(1)}, f32[16,128]{1,0:T(8,128)S(1)}, f32[16,128]{1,0:T(8,128)S(1)}) custom-call(f32[4,1,1152]{2,1,0:T(1,128)S(1)} %all_to_all.62.z, bf16[64,6144]{1,0:T(8,128)(2,1)S(1)} %reshape.27.src, bf16[64,6144]{1,0:T(8,128)(2,1)S(1)} %reshape.35.tgt, ...), custom_call_target="tpu_custom_call" | custom-call | tf_op jit(solution)/shard_map/pallas_call | solution.py:248
  87.3 12.5 %all_to_all.63.y = bf16[32,16,128]{2,1,0:T(8,128)(2,1)S(1)} all-to-all(bf16[32,16,128]{2,1,0:T(8,128)(2,1)S(1)} %get-tuple-element.18), channel_id=1, replica_groups=mesh['row_0'=4,'row_1'=2,'core'=2,'col_0'=8,'col_1'=4] {'col_0','col_1'}, dimensions={0} | all-to-all | bytes 262144 | tf_op jit(solution)/shard_map/all_to_all | solution.py:259
  99.8 1.2 shard_map.126
  101.0 12.4 %all_to_all.64.y = bf16[16,16,128]{2,1,0:T(8,128)(2,1)S(1)} all-to-all(bf16[16,16,128]{2,1,0:T(8,128)(2,1)S(1)} %shard_map.126), channel_id=1, replica_groups=mesh['row_0'=4,'row_1'=2,'core'=2,'col_0'=8,'col_1'=4] {'row_0','row_1',..., dimensions={0} | all-to-all | bytes 131072 | tf_op jit(solution)/shard_map/all_to_all | solution.py:259
  113.4 1.2 shard_map.127
  114.6 12.7 %all_to_all.65.y = bf16[32,16,128]{2,1,0:T(8,128)(2,1)S(1)} all-to-all(bf16[32,16,128]{2,1,0:T(8,128)(2,1)S(1)} %shard_map.127), channel_id=1, replica_groups=mesh['row_0'=4,'row_1'=2,'core'=2,'col_0'=8,'col_1'=4] {'col_0','col_1'}, dimensions={0} | all-to-all | bytes 262144 | tf_op jit(solution)/shard_map/all_to_all | solution.py:259
  127.4 1.2 shard_map.128
  128.6 11.9 %all_to_all.66.y = bf16[16,16,128]{2,1,0:T(8,128)(2,1)S(1)} all-to-all(bf16[16,16,128]{2,1,0:T(8,128)(2,1)S(1)} %shard_map.128), channel_id=1, replica_groups=mesh['row_0'=4,'row_1'=2,'core'=2,'col_0'=8,'col_1'=4] {'row_0','row_1',..., dimensions={0} | all-to-all | bytes 131072 | tf_op jit(solution)/shard_map/all_to_all | solution.py:259
  140.4 1.2 shard_map.129
  141.7 12.8 %all_to_all.67.y = bf16[32,16,128]{2,1,0:T(8,128)(2,1)S(1)} all-to-all(bf16[32,16,128]{2,1,0:T(8,128)(2,1)S(1)} %shard_map.129), channel_id=1, replica_groups=mesh['row_0'=4,'row_1'=2,'core'=2,'col_0'=8,'col_1'=4] {'col_0','col_1'}, dimensions={0} | all-to-all | bytes 262144 | tf_op jit(solution)/shard_map/all_to_all | solution.py:259
  154.5 1.9 shard_map.130
  156.3 4.9 %all-to-all-start.9 = ((bf16[16,16,128]{2,1,0:T(8,128)(2,1)}), bf16[16,16,128]{2,1,0:T(8,128)(2,1)S(1)}, u32[]{:S(2)}, u32[]{:S(2)}) async-start(bf16[16,16,128]{2,1,0:T(8,128)(2,1)} %get-tuple-element.25), calls=%async_computation.9 | async-start | bytes 131072 | tf_op jit(solution)/shard_map/all_to_all | solution.py:259
  161.2 3.4 %copy-done.1 = bf16[2048,2048]{1,0:T(8,128)(2,1)S(1)} copy-done((bf16[2048,2048]{1,0:T(8,128)(2,1)S(1)}, bf16[2048,2048]{1,0:T(8,128)(2,1)}, u32[]{:S(2)}) %copy-start.1) | copy-done | bytes 8388632
  164.6 2.3 %shard_map.131 = (f32[16,128]{1,0:T(8,128)}, f32[64,2048]{1,0:T(8,128)S(1)}) custom-call(f32[16,128]{1,0:T(8,128)S(1)} %get-tuple-element.23.row_scale, bf16[2048,2048]{1,0:T(8,128)(2,1)S(1)} %copy-done.1, bf16[64,6144]{1,0:T(8,128)(2,1)S(1)} %reshape.27.src), custom_call_target="tpu_custom_call" | custom-call | tf_op jit(solution)/shard_map/pallas_call | solution.py:248
  166.9 2.2 %all-to-all-done.9.y = bf16[16,16,128]{2,1,0:T(8,128)(2,1)S(1)} async-done(((bf16[16,16,128]{2,1,0:T(8,128)(2,1)}), bf16[16,16,128]{2,1,0:T(8,128)(2,1)S(1)}, u32[]{:S(2)}, u32[]{:S(2)}) %all-to-all-start.9) | async-done | bytes 65568 | tf_op jit(solution)/shard_map/all_to_all | solution.py:259
  170.0 13.8 %all_to_all.68.y = bf16[16,32,128]{2,1,0:T(8,128)(2,1)S(1)} all-to-all(bf16[16,32,128]{2,1,0:T(8,128)(2,1)S(1)} %get-tuple-element.28), channel_id=1, replica_groups=mesh['row_0'=4,'row_1'=2,'core'=2,'col_0'=8,'col_1'=4] {'row_0','row_1',..., dimensions={0} | all-to-all | bytes 262144 | tf_op jit(solution)/shard_map/all_to_all | solution.py:259
  183.8 15.3 %all_to_all.69.y = bf16[32,32,128]{2,1,0:T(8,128)(2,1)S(1)} all-to-all(bf16[32,32,128]{2,1,0:T(8,128)(2,1)S(1)} %shard_map.133), channel_id=1, replica_groups=mesh['row_0'=4,'row_1'=2,'core'=2,'col_0'=8,'col_1'=4] {'col_0','col_1'}, dimensions={0} | all-to-all | bytes 524288 | tf_op jit(solution)/shard_map/all_to_all | solution.py:259
  (11 shorter events, 2.6 us)
Async XLA Ops:
  2.4 34.8 %all-to-all-start = ((bf16[32,2,6144]{2,1,0:T(2,128)(2,1)}), bf16[32,2,6144]{2,1,0:T(2,128)(2,1)S(1)}, u32[]{:S(2)}, u32[]{:S(2)}) async-start(bf16[32,2,6144]{2,1,0:T(2,128)(2,1)} %get-tuple-element.16), calls=%async_computation | async-start | bytes 1572864 | tf_op jit(solution)/shard_map/all_to_all | solution.py:259
  87.3 67.2 %copy-start = (bf16[2048,2048]{1,0:T(8,128)(2,1)}, bf16[2048,2048]{1,0:T(8,128)(2,1)S(1)}, u32[]{:S(2)}) copy-start(bf16[2048,2048]{1,0:T(8,128)(2,1)S(1)} %get-tuple-element.20.kernel) | copy-start | bytes 25165828
  156.3 12.8 %all-to-all-start.9 = ((bf16[16,16,128]{2,1,0:T(8,128)(2,1)}), bf16[16,16,128]{2,1,0:T(8,128)(2,1)S(1)}, u32[]{:S(2)}, u32[]{:S(2)}) async-start(bf16[16,16,128]{2,1,0:T(8,128)(2,1)} %get-tuple-element.25), calls=%async_computation.9 | async-start | bytes 131072 | tf_op jit(solution)/shard_map/all_to_all | solution.py:259
  161.2 3.4 %copy-start.1 = (bf16[2048,2048]{1,0:T(8,128)(2,1)S(1)}, bf16[2048,2048]{1,0:T(8,128)(2,1)}, u32[]{:S(2)}) copy-start(bf16[2048,2048]{1,0:T(8,128)(2,1)} %copy-done) | copy-start | bytes 25165828

commit v5 on v4

--- a/solution.py
+++ b/solution.py
@@ -63,15 +63,6 @@
     for s in range(tile_ref.shape[0]):
         tile_ref[s : s + 1, :] = row[:, s * LANES : (s + 1) * LANES]
     return tile_ref[...]
-
-
-def over_lanes(v):
-    width = v.shape[1]
-    total = v[:, :LANES]
-    for s in range(1, width // LANES):
-        total = total + v[:, s * LANES : (s + 1) * LANES]
-    ones = jnp.ones((PAD, LANES), BF16)
-    return sum(dot(ones, part.astype(BF16), LAST)[0:1] for part in three_parts(total))
 
 
 def send(out_ref, v):
@@ -132,10 +123,11 @@
         copy.wait()
     xs[rank:] = logit_rows(src_logit[...], True)
     xt[rank:] = logit_rows(tgt_logit[...], False)
-    tile = jnp.exp(dot(xs[...], xt[...], FIRST)).astype(BF16)
     row = lax.broadcasted_iota(jnp.int32, (PAD, n), 0)
     left = jnp.concatenate([src[:, 2 * n :], jnp.where(row == 0, 1.0, 0.0).astype(BF16)], axis=0)
-    both = in_parts(dot(left, tile, PLAIN), right[...])
+    tile = jnp.exp(dot(xs[...], xt[...], FIRST)).astype(BF16)
+    side = dot(left, tile, PLAIN)
+    both = in_parts(side, right[...])
     core = halves_on_lanes(both[:, : 2 * rank], rank)
     total = both[rank : rank + 1, 2 * rank : 2 * rank + 1]
     src_sum = jnp.sum(src_weight[...], keepdims=True)
@@ -162,7 +154,7 @@
     mass_scale, row_peers, col_peers,
     z, src, tgt, src_logit_in, tgt_logit_in, src_weight_in, tgt_weight_in,
     kernel, flipped, out, row_mass, col_mass,
-    xs, xt, tiles, core, src_logit, tgt_logit, src_weight, tgt_weight, sem,
+    xs, xt, totals, tiles, core, src_logit, tgt_logit, src_weight, tgt_weight, sem,
 ):
     copies = fetch(
         (src_logit_in, tgt_logit_in, src_weight_in, tgt_weight_in),
@@ -198,8 +190,10 @@
     xt[2 * rank :] = logit_rows(tgt_logit[...] - jnp.log(grand_total), False)
     tile = jnp.exp(dot(xs[...], xt[...], FIRST)).astype(BF16)
     kernel[...] = tile
-    flipped[...] = tile.T
-    send(out, to_tiles(over_lanes(tile.astype(F32)), tiles))
+    turned = tile.T
+    flipped[...] = turned
+    totals[...] = dot(jnp.ones((8, m), BF16), turned, PLAIN)
+    send(out, to_tiles(totals[0:1], tiles))
 
 
 def sweep_kernel(y, mass, kernel, out, *rest):
@@ -211,14 +205,23 @@
     send(out, to_tiles(dot(weights, kernel[...], PLAIN)[0:1], tiles))
 
 
-def side_kernel(shift, row_scale, kernel, src, row_potential, side, flat):
+def side_kernel(shift, row_scale, src, kernel, row_potential, side, flat, tile, sem):
     rank = src.shape[0]
-    n = kernel.shape[0]
+    slabs, rows, _ = tile.shape
+    n = slabs * rows
+    copies = fetch(
+        [kernel.at[pl.ds(k * rows, rows)] for k in range(slabs)],
+        [tile.at[k] for k in range(slabs)],
+        sem,
+    )
     row_potential[...] = jnp.log(row_scale[...]) + shift
-    rows = to_lanes(row_scale[...], flat)
-    left = src[:, 2 * n :].astype(F32) * rows[0:1]
+    scale = to_lanes(row_scale[...], flat)
+    left = src[:, 2 * n :].astype(F32) * scale[0:1]
     parts = jnp.concatenate(three_parts(left), axis=0).astype(BF16)
-    total = dot(parts, kernel[...], PLAIN)
+    total = 0.0
+    for k, copy in enumerate(copies):
+        copy.wait()
+        total = total + dot(parts[:, k * rows : (k + 1) * rows], tile[k], PLAIN)
     side[...] = total[:rank] + total[rank : 2 * rank] + total[2 * rank :]
 
 
@@ -329,6 +332,7 @@
         [
             ((2 * rank + PAD, n), BF16),
             ((2 * rank + PAD, m), BF16),
+            ((8, n), F32),
             ((nt, LANES), F32),
             ((half, LANES), F32),
             ((1, n), F32),
@@ -360,8 +364,8 @@
     row_potential, side = call(
         functools.partial(side_kernel, math.log(n_all) + math.log(m_all)),
         [((nt, LANES), F32), ((rank, m), F32)],
-        [((8, n), F32)],
-        row_scale, kernel, src,
+        [((8, n), F32), ((8, n // 8, m), BF16), pltpu.SemaphoreType.DMA((8,))],
+        row_scale, src, kernel, stay=1, room=16,
     )
     col_potential, part = call(
         closing_kernel,

time: 201 us -> 199 us (0.990)
  local copies, waits for them, and re-layouts: 3.85 us -> 0.48 us
    unnamed x5 -> x3, local copies, waits for them, and re-layouts: 3.56 us -> 0.18 us
  transfers between devices with their start and end apart: 2 -> 2, of which waited for: 2 -> 2; matrix products, arithmetic and copies ran while one was open for 0% -> 0% of each run, Pallas kernels for 1% -> 2%
where the time goes in v5:
time: 199 us; the launch traced here: 198 us
  blocking collectives  150 us (75%)
  Pallas kernels  24.3 us (12%)
  starting transfers between devices  18.6 us (9%)
  waiting for transfers between devices  4.1 us (2%)
    all_to_all x10, blocking collectives, exchange(): return lax.all_to_all(value, axis, 0, 0, tiled=True)  129 us
    pallas_call x14, Pallas kernels, call(): pl.pallas_call(body, out_shape=[jax.ShapeDtypeStruct(s, d) for s, d in ou...  24.3 us
    all_gather x1, blocking collectives, body(): tgt = lax.all_gather(tgt, ROW, axis=0, tiled=True)  20.5 us
    all_to_all x2, starting transfers between devices, exchange(): return lax.all_to_all(value, axis, 0, 0, tiled=True)  18.6 us
    all_to_all x2, waiting for transfers between devices, exchange(): return lax.all_to_all(value, axis, 0, 0, tiled=True)  4.1 us
  transfers between devices with their start and end apart: 2, of which 2 were waited for; matrix products, arithmetic and copies ran while one was open for 0% of the time, Pallas kernels for 2%

profile of v5, /device:TPU:1, one launch (start us, length us, event | category | flops | bytes accessed | tf_op | source)
XLA Modules:
  0.0 198.0 jit_solution(6351546569967721713)
XLA Ops:
  0.6 1.8 shard_map.121
  2.4 13.7 %all-to-all-start = ((bf16[32,2,6144]{2,1,0:T(2,128)(2,1)}), bf16[32,2,6144]{2,1,0:T(2,128)(2,1)S(1)}, u32[]{:S(2)}, u32[]{:S(2)}) async-start(bf16[32,2,6144]{2,1,0:T(2,128)(2,1)} %get-tuple-element.16), calls=%async_computation | async-start | bytes 1572864 | tf_op jit(solution)/shard_map/all_to_all | solution.py:262
  16.2 20.5 %all-gather = bf16[16,4,6144]{2,1,0:T(4,128)(2,1)S(1)} all-gather(bf16[1,4,6144]{2,1,0:T(4,128)(2,1)S(1)} %bitcast.7), channel_id=1, replica_groups=mesh['row_0'=4,'row_1'=2,'core'=2,'col_0'=8,'col_1'=4] {'row_0','row_1',..., dimensions={0}, use_global_device_ids=true | all-gather | bytes 835584 | tf_op jit(solution)/shard_map/all_gather | solution.py:299
  37.5 5.0 %shard_map.122 = f32[16,1,1152]{2,1,0:T(1,128)S(1)} custom-call(bf16[64,6144]{1,0:T(8,128)(2,1)S(1)} %reshape.27.src, bf16[64,6144]{1,0:T(8,128)(2,1)S(1)} %reshape.35.tgt, f32[1,2048]{1,0:T(1,128)} %bitcast.8, f32[1,2048]{1,0:T(1,128)} %bitcast.10, f32[16,128]{1,0:T(8,128)} %bitcast.12, f32[16,128]{1,0:T(8,128)} %bitcast.14), custom_call_target="tpu_custom_call" | custom-call | tf_op jit(solution)/shard_map/pallas_call | solution.py:251
  42.5 17.6 %all_to_all.60.y = f32[16,1,1152]{2,1,0:T(1,128)S(1)} all-to-all(f32[16,1,1152]{2,1,0:T(1,128)S(1)} %shard_map.122), channel_id=1, replica_groups=mesh['row_0'=4,'row_1'=2,'core'=2,'col_0'=8,'col_1'=4] {'row_0','row_1',..., dimensions={0} | all-to-all | bytes 147456 | tf_op jit(solution)/shard_map/all_to_all | solution.py:262
  60.2 14.7 %all_to_all.61.y = f32[32,1,1152]{2,1,0:T(1,128)S(1)} all-to-all(f32[32,1,1152]{2,1,0:T(1,128)S(1)} %shard_map.123), channel_id=1, replica_groups=mesh['row_0'=4,'row_1'=2,'core'=2,'col_0'=8,'col_1'=4] {'col_0','col_1'}, dimensions={0} | all-to-all | bytes 294912 | tf_op jit(solution)/shard_map/all_to_all | solution.py:262
  74.9 7.0 %all_to_all.62.z = f32[4,1,1152]{2,1,0:T(1,128)S(1)} all-to-all(f32[4,1,1152]{2,1,0:T(1,128)S(1)} %shard_map.124), channel_id=1, replica_groups=mesh['row_0'=4,'row_1'=2,'core'=2,'col_0'=8,'col_1'=4] {'row_1','core'}, dimensions={0} | all-to-all | bytes 36864 | tf_op jit(solution)/shard_map/all_to_all | solution.py:262
  82.0 5.1 %shard_map.125 = (bf16[2048,2048]{1,0:T(8,128)(2,1)S(1)}, bf16[2048,2048]{1,0:T(8,128)(2,1)S(1)}, bf16[32,16,128]{2,1,0:T(8,128)(2,1)S(1)}, f32[16,128]{1,0:T(8,128)S(1)}, f32[16,128]{1,0:T(8,128)S(1)}) custom-call(f32[4,1,1152]{2,1,0:T(1,128)S(1)} %all_to_all.62.z, bf16[64,6144]{1,0:T(8,128)(2,1)S(1)} %reshape.27.src, bf16[64,6144]{1,0:T(8,128)(2,1)S(1)} %reshape.35.tgt, ...), custom_call_target="tpu_custom_call" | custom-call | tf_op jit(solution)/shard_map/pallas_call | solution.py:251
  87.1 12.5 %all_to_all.63.y = bf16[32,16,128]{2,1,0:T(8,128)(2,1)S(1)} all-to-all(bf16[32,16,128]{2,1,0:T(8,128)(2,1)S(1)} %get-tuple-element.18), channel_id=1, replica_groups=mesh['row_0'=4,'row_1'=2,'core'=2,'col_0'=8,'col_1'=4] {'col_0','col_1'}, dimensions={0} | all-to-all | bytes 262144 | tf_op jit(solution)/shard_map/all_to_all | solution.py:262
  99.6 1.2 shard_map.126
  100.8 12.4 %all_to_all.64.y = bf16[16,16,128]{2,1,0:T(8,128)(2,1)S(1)} all-to-all(bf16[16,16,128]{2,1,0:T(8,128)(2,1)S(1)} %shard_map.126), channel_id=1, replica_groups=mesh['row_0'=4,'row_1'=2,'core'=2,'col_0'=8,'col_1'=4] {'row_0','row_1',..., dimensions={0} | all-to-all | bytes 131072 | tf_op jit(solution)/shard_map/all_to_all | solution.py:262
  113.2 1.2 shard_map.127
  114.4 12.7 %all_to_all.65.y = bf16[32,16,128]{2,1,0:T(8,128)(2,1)S(1)} all-to-all(bf16[32,16,128]{2,1,0:T(8,128)(2,1)S(1)} %shard_map.127), channel_id=1, replica_groups=mesh['row_0'=4,'row_1'=2,'core'=2,'col_0'=8,'col_1'=4] {'col_0','col_1'}, dimensions={0} | all-to-all | bytes 262144 | tf_op jit(solution)/shard_map/all_to_all | solution.py:262
  127.2 1.2 shard_map.128
  128.4 11.9 %all_to_all.66.y = bf16[16,16,128]{2,1,0:T(8,128)(2,1)S(1)} all-to-all(bf16[16,16,128]{2,1,0:T(8,128)(2,1)S(1)} %shard_map.128), channel_id=1, replica_groups=mesh['row_0'=4,'row_1'=2,'core'=2,'col_0'=8,'col_1'=4] {'row_0','row_1',..., dimensions={0} | all-to-all | bytes 131072 | tf_op jit(solution)/shard_map/all_to_all | solution.py:262
  140.2 1.2 shard_map.129
  141.5 12.8 %all_to_all.67.y = bf16[32,16,128]{2,1,0:T(8,128)(2,1)S(1)} all-to-all(bf16[32,16,128]{2,1,0:T(8,128)(2,1)S(1)} %shard_map.129), channel_id=1, replica_groups=mesh['row_0'=4,'row_1'=2,'core'=2,'col_0'=8,'col_1'=4] {'col_0','col_1'}, dimensions={0} | all-to-all | bytes 262144 | tf_op jit(solution)/shard_map/all_to_all | solution.py:262
  154.3 1.8 shard_map.130
  156.1 4.9 %all-to-all-start.9 = ((bf16[16,16,128]{2,1,0:T(8,128)(2,1)}), bf16[16,16,128]{2,1,0:T(8,128)(2,1)S(1)}, u32[]{:S(2)}, u32[]{:S(2)}) async-start(bf16[16,16,128]{2,1,0:T(8,128)(2,1)} %get-tuple-element.25), calls=%async_computation.9 | async-start | bytes 131072 | tf_op jit(solution)/shard_map/all_to_all | solution.py:262
  161.0 4.1 %shard_map.131 = (f32[16,128]{1,0:T(8,128)}, f32[64,2048]{1,0:T(8,128)S(1)}) custom-call(f32[16,128]{1,0:T(8,128)S(1)} %get-tuple-element.23.row_scale, bf16[64,6144]{1,0:T(8,128)(2,1)S(1)} %reshape.27.src, bf16[2048,2048]{1,0:T(8,128)(2,1)} %copy-done), custom_call_target="tpu_custom_call" | custom-call | tf_op jit(solution)/shard_map/pallas_call | solution.py:251
  165.1 3.7 %all-to-all-done.9.y = bf16[16,16,128]{2,1,0:T(8,128)(2,1)S(1)} async-done(((bf16[16,16,128]{2,1,0:T(8,128)(2,1)}), bf16[16,16,128]{2,1,0:T(8,128)(2,1)S(1)}, u32[]{:S(2)}, u32[]{:S(2)}) %all-to-all-start.9) | async-done | bytes 65568 | tf_op jit(solution)/shard_map/all_to_all | solution.py:262
  168.9 0.9 shard_map.132
  169.8 12.2 %all_to_all.68.y = bf16[16,32,128]{2,1,0:T(8,128)(2,1)S(1)} all-to-all(bf16[16,32,128]{2,1,0:T(8,128)(2,1)S(1)} %get-tuple-element.28), channel_id=1, replica_groups=mesh['row_0'=4,'row_1'=2,'core'=2,'col_0'=8,'col_1'=4] {'row_0','row_1',..., dimensions={0} | all-to-all | bytes 262144 | tf_op jit(solution)/shard_map/all_to_all | solution.py:262
  182.0 15.3 %all_to_all.69.y = bf16[32,32,128]{2,1,0:T(8,128)(2,1)S(1)} all-to-all(bf16[32,32,128]{2,1,0:T(8,128)(2,1)S(1)} %shard_map.133), channel_id=1, replica_groups=mesh['row_0'=4,'row_1'=2,'core'=2,'col_0'=8,'col_1'=4] {'col_0','col_1'}, dimensions={0} | all-to-all | bytes 524288 | tf_op jit(solution)/shard_map/all_to_all | solution.py:262
  (9 shorter events, 1.7 us)
Async XLA Ops:
  2.4 34.8 %all-to-all-start = ((bf16[32,2,6144]{2,1,0:T(2,128)(2,1)}), bf16[32,2,6144]{2,1,0:T(2,128)(2,1)S(1)}, u32[]{:S(2)}, u32[]{:S(2)}) async-start(bf16[32,2,6144]{2,1,0:T(2,128)(2,1)} %get-tuple-element.16), calls=%async_computation | async-start | bytes 1572864 | tf_op jit(solution)/shard_map/all_to_all | solution.py:262
  87.1 67.2 %copy-start = (bf16[2048,2048]{1,0:T(8,128)(2,1)}, bf16[2048,2048]{1,0:T(8,128)(2,1)S(1)}, u32[]{:S(2)}) copy-start(bf16[2048,2048]{1,0:T(8,128)(2,1)S(1)} %get-tuple-element.20.kernel) | copy-start | bytes 25165828
  156.1 12.8 %all-to-all-start.9 = ((bf16[16,16,128]{2,1,0:T(8,128)(2,1)}), bf16[16,16,128]{2,1,0:T(8,128)(2,1)S(1)}, u32[]{:S(2)}, u32[]{:S(2)}) async-start(bf16[16,16,128]{2,1,0:T(8,128)(2,1)} %get-tuple-element.25), calls=%async_computation.9 | async-start | bytes 131072 | tf_op jit(solution)/shard_map/all_to_all | solution.py:262

commit v6 on v5

--- a/solution.py
+++ b/solution.py
@@ -101,19 +101,17 @@
     tgt_out[...] = jnp.concatenate([ref[...] for ref in here[3:]], axis=1)
 
 
-def opening_kernel(
-    src, tgt, src_logit_in, tgt_logit_in, src_weight_in, tgt_weight_in, out,
-    xs, xt, right, src_logit, tgt_logit, src_weight, tgt_weight, flat, sem,
+def prepare_kernel(
+    tgt, src_logit_in, tgt_logit_in, src_weight_in, tgt_weight_in,
+    xt, right, src_rows, tgt_logit, src_weight, tgt_weight, sums, src_logit, sem,
 ):
     copies = fetch(
         (src_logit_in, tgt_logit_in, src_weight_in, tgt_weight_in),
         (src_logit, tgt_logit, src_weight, tgt_weight),
         sem,
     )
-    rank = src.shape[0]
-    n = src_logit.shape[1]
+    rank = tgt.shape[0]
     m = tgt_logit.shape[1]
-    xs[:rank] = (src[:, :n].astype(F32) * 0.125).astype(BF16)
     xt[:rank] = tgt[:, :m]
     right[:rank] = tgt[:, 2 * m :]
     right[rank : 2 * rank] = tgt[:, 2 * m :]
@@ -121,8 +119,19 @@
     right[2 * rank :] = jnp.where(row == 0, 1.0, 0.0).astype(BF16)
     for copy in copies:
         copy.wait()
-    xs[rank:] = logit_rows(src_logit[...], True)
+    src_rows[...] = logit_rows(src_logit[...], True)
     xt[rank:] = logit_rows(tgt_logit[...], False)
+    src_sum = jnp.sum(src_weight[...], keepdims=True)
+    tgt_sum = jnp.sum(tgt_weight[...], keepdims=True)
+    lane = lax.broadcasted_iota(jnp.int32, (1, LANES), 1)
+    sums[...] = jnp.where(lane == 1, src_sum, jnp.where(lane == 2, tgt_sum, 0.0))
+
+
+def opening_kernel(src, xt, right, src_rows, known, out, xs, flat):
+    rank = src.shape[0]
+    n = src_rows.shape[1]
+    xs[:rank] = (src[:, :n].astype(F32) * 0.125).astype(BF16)
+    xs[rank:] = src_rows[...]
     row = lax.broadcasted_iota(jnp.int32, (PAD, n), 0)
     left = jnp.concatenate([src[:, 2 * n :], jnp.where(row == 0, 1.0, 0.0).astype(BF16)], axis=0)
     tile = jnp.exp(dot(xs[...], xt[...], FIRST)).astype(BF16)
@@ -130,12 +139,8 @@
     both = in_parts(side, right[...])
     core = halves_on_lanes(both[:, : 2 * rank], rank)
     total = both[rank : rank + 1, 2 * rank : 2 * rank + 1]
-    src_sum = jnp.sum(src_weight[...], keepdims=True)
-    tgt_sum = jnp.sum(tgt_weight[...], keepdims=True)
     lane = lax.broadcasted_iota(jnp.int32, (1, LANES), 1)
-    sums = jnp.where(
-        lane == 0, total, jnp.where(lane == 1, src_sum, jnp.where(lane == 2, tgt_sum, 0.0))
-    )
+    sums = jnp.where(lane == 0, total, known[...])
     parts, _, width = flat.shape
     for q in range(parts):
         for s in range(width // LANES - 1):
@@ -152,18 +157,13 @@
 
 def tile_kernel(
     mass_scale, row_peers, col_peers,
-    z, src, tgt, src_logit_in, tgt_logit_in, src_weight_in, tgt_weight_in,
+    z, src, tgt, src_rows, tgt_logit, src_weight, tgt_weight,
     kernel, flipped, out, row_mass, col_mass,
-    xs, xt, totals, tiles, core, src_logit, tgt_logit, src_weight, tgt_weight, sem,
+    xs, xt, totals, tiles, core,
 ):
-    copies = fetch(
-        (src_logit_in, tgt_logit_in, src_weight_in, tgt_weight_in),
-        (src_logit, tgt_logit, src_weight, tgt_weight),
-        sem,
-    )
     rank = src.shape[0]
     half = rank // 2
-    n = src_logit.shape[1]
+    n = src_rows.shape[1]
     m = tgt_logit.shape[1]
     parts, _, width = z.shape
     for q in range(parts):
@@ -180,11 +180,9 @@
     bottom = dot(parts, jnp.concatenate([bottom, bottom, bottom], axis=0), FIRST)
     xs[:rank] = (src[:, :n].astype(F32) * 0.125).astype(BF16)
     xs[rank : 2 * rank] = (2.0 * (top[:rank] + bottom[rank:])).astype(BF16)
-    for copy in copies:
-        copy.wait()
     row_mass[...] = src_weight[...] / (sums[:, 1:2] / col_peers)
     col_mass[...] = tgt_weight[...] / (sums[:, 2:3] / row_peers)
-    xs[2 * rank :] = logit_rows(src_logit[...], True)
+    xs[2 * rank :] = src_rows[...]
     xt[:rank] = tgt[:, :m]
     xt[rank : 2 * rank] = tgt[:, m : 2 * m]
     xt[2 * rank :] = logit_rows(tgt_logit[...] - jnp.log(grand_total), False)
@@ -302,21 +300,25 @@
 
     near = lax.axis_size(NEAR)
     width = half * LANES // near + LANES
+    xt, right, src_rows, tgt_logit, src_weight, tgt_weight, known = call(
+        prepare_kernel,
+        [
+            ((rank + PAD, m), BF16),
+            ((2 * rank + PAD, m), BF16),
+            ((PAD, n), BF16),
+            ((1, m), F32),
+            ((nt, LANES), F32),
+            ((mt, LANES), F32),
+            ((1, LANES), F32),
+        ],
+        [((1, n), F32), pltpu.SemaphoreType.DMA((4,))],
+        tgt, src_logit, tgt_logit, src_weight, tgt_weight, stay=4,
+    )
     (part,) = call(
         opening_kernel,
         [((row_peers, 1, width), F32)],
-        [
-            ((rank + PAD, n), BF16),
-            ((rank + PAD, m), BF16),
-            ((2 * rank + PAD, m), BF16),
-            ((1, n), F32),
-            ((1, m), F32),
-            ((nt, LANES), F32),
-            ((mt, LANES), F32),
-            ((near, 1, width), F32),
-            pltpu.SemaphoreType.DMA((4,)),
-        ],
-        src, tgt, src_logit, tgt_logit, src_weight, tgt_weight, stay=4, room=32,
+        [((rank + PAD, n), BF16), ((near, 1, width), F32)],
+        src, xt, right, src_rows, known, room=32,
     )
     (part,) = call(relay_kernel, [((col_peers, 1, width), F32)], [], exchange(part, ROW))
     (part,) = call(relay_kernel, [((near, 1, width), F32)], [], exchange(part, COL))
@@ -335,14 +337,8 @@
             ((8, n), F32),
             ((nt, LANES), F32),
             ((half, LANES), F32),
-            ((1, n), F32),
-            ((1, m), F32),
-            ((nt, LANES), F32),
-            ((mt, LANES), F32),
-            pltpu.SemaphoreType.DMA((4,)),
-        ],
-        exchange(part, NEAR), src, tgt, src_logit, tgt_logit, src_weight, tgt_weight,
-        stay=4, room=32,
+        ],
+        exchange(part, NEAR), src, tgt, src_rows, tgt_logit, src_weight, tgt_weight, room=32,
     )
     for sweep in range(SWEEPS):
         last = sweep + 1 == SWEEPS

time: 199 us -> 198 us (level)
    pallas_call x14 -> x15, Pallas kernels: 24.3 us -> 24 us  [call(): pl.pallas_call(body, out_shape=[jax.ShapeDtypeStruct(s, d) for s, d in ou...]
  transfers between devices with their start and end apart: 2 -> 2, of which waited for: 2 -> 1; matrix products, arithmetic and copies ran while one was open for 0% -> 0% of each run, Pallas kernels for 2% -> 3%
where the time goes in v6:
time: 198 us; the launch traced here: 197 us
  blocking collectives  149 us (75%)
  Pallas kernels  24 us (12%)
  starting transfers between devices  18.6 us (9%)
  waiting for transfers between devices  3.75 us (2%)
    all_to_all x10, blocking collectives, exchange(): return lax.all_to_all(value, axis, 0, 0, tiled=True)  129 us
    pallas_call x15, Pallas kernels, call(): pl.pallas_call(body, out_shape=[jax.ShapeDtypeStruct(s, d) for s, d in ou...  24 us
    all_gather x1, blocking collectives, body(): tgt = lax.all_gather(tgt, ROW, axis=0, tiled=True)  20.5 us
    all_to_all x2, starting transfers between devices, exchange(): return lax.all_to_all(value, axis, 0, 0, tiled=True)  18.6 us
  transfers between devices with their start and end apart: 2, of which 1 were waited for; matrix products, arithmetic and copies ran while one was open for 0% of the time, Pallas kernels for 3%

profile of v6, /device:TPU:1, one launch (start us, length us, event | category | flops | bytes accessed | tf_op | source)
XLA Modules:
  0.0 196.8 jit_solution(3230328003895560040)
XLA Ops:
  0.6 1.8 shard_map.121
  2.4 13.7 %all-to-all-start = ((bf16[32,2,6144]{2,1,0:T(2,128)(2,1)}), bf16[32,2,6144]{2,1,0:T(2,128)(2,1)S(1)}, u32[]{:S(2)}, u32[]{:S(2)}) async-start(bf16[32,2,6144]{2,1,0:T(2,128)(2,1)} %get-tuple-element.23), calls=%async_computation | async-start | bytes 1572864 | tf_op jit(solution)/shard_map/all_to_all | solution.py:260
  16.2 20.5 %all-gather = bf16[16,4,6144]{2,1,0:T(4,128)(2,1)S(1)} all-gather(bf16[1,4,6144]{2,1,0:T(4,128)(2,1)S(1)} %bitcast.7), channel_id=1, replica_groups=mesh['row_0'=4,'row_1'=2,'core'=2,'col_0'=8,'col_1'=4] {'row_0','row_1',..., dimensions={0}, use_global_device_ids=true | all-gather | bytes 835584 | tf_op jit(solution)/shard_map/all_gather | solution.py:297
  36.9 0.9 shard_map.122
  38.1 4.1 %shard_map.123 = f32[16,1,1152]{2,1,0:T(1,128)S(1)} custom-call(bf16[64,6144]{1,0:T(8,128)(2,1)S(1)} %reshape.27.src, bf16[80,2048]{1,0:T(8,128)(2,1)S(1)} %get-tuple-element.25.xt, bf16[144,2048]{1,0:T(8,128)(2,1)S(1)} %get-tuple-element.26.right, bf16[16,2048]{1,0:T(8,128)(2,1)S(1)} %get-tuple-element.27.src_rows, f32[1,128]{1,0:T(1,128)S(1)} %get-tuple-element.28.known), custom_call_target="tpu_custom_call" | custom-call | tf_op jit(solution)/shard_map/pallas_call | solution.py:249
  42.2 17.0 %all_to_all.60.y = f32[16,1,1152]{2,1,0:T(1,128)S(1)} all-to-all(f32[16,1,1152]{2,1,0:T(1,128)S(1)} %shard_map.123), channel_id=1, replica_groups=mesh['row_0'=4,'row_1'=2,'core'=2,'col_0'=8,'col_1'=4] {'row_0','row_1',..., dimensions={0} | all-to-all | bytes 147456 | tf_op jit(solution)/shard_map/all_to_all | solution.py:260
  59.3 14.7 %all_to_all.61.y = f32[32,1,1152]{2,1,0:T(1,128)S(1)} all-to-all(f32[32,1,1152]{2,1,0:T(1,128)S(1)} %shard_map.124), channel_id=1, replica_groups=mesh['row_0'=4,'row_1'=2,'core'=2,'col_0'=8,'col_1'=4] {'col_0','col_1'}, dimensions={0} | all-to-all | bytes 294912 | tf_op jit(solution)/shard_map/all_to_all | solution.py:260
  74.1 7.0 %all_to_all.62.z = f32[4,1,1152]{2,1,0:T(1,128)S(1)} all-to-all(f32[4,1,1152]{2,1,0:T(1,128)S(1)} %shard_map.125), channel_id=1, replica_groups=mesh['row_0'=4,'row_1'=2,'core'=2,'col_0'=8,'col_1'=4] {'row_1','core'}, dimensions={0} | all-to-all | bytes 36864 | tf_op jit(solution)/shard_map/all_to_all | solution.py:260
  81.1 4.7 %shard_map.126 = (bf16[2048,2048]{1,0:T(8,128)(2,1)S(1)}, bf16[2048,2048]{1,0:T(8,128)(2,1)S(1)}, bf16[32,16,128]{2,1,0:T(8,128)(2,1)S(1)}, f32[16,128]{1,0:T(8,128)S(1)}, f32[16,128]{1,0:T(8,128)S(1)}) custom-call(f32[4,1,1152]{2,1,0:T(1,128)S(1)} %all_to_all.62.z, bf16[64,6144]{1,0:T(8,128)(2,1)S(1)} %reshape.27.src, bf16[64,6144]{1,0:T(8,128)(2,1)S(1)} %reshape.35.tgt, ...), custom_call_target="tpu_custom_call" | custom-call | tf_op jit(solution)/shard_map/pallas_call | solution.py:249
  85.8 12.5 %all_to_all.63.y = bf16[32,16,128]{2,1,0:T(8,128)(2,1)S(1)} all-to-all(bf16[32,16,128]{2,1,0:T(8,128)(2,1)S(1)} %get-tuple-element.32), channel_id=1, replica_groups=mesh['row_0'=4,'row_1'=2,'core'=2,'col_0'=8,'col_1'=4] {'col_0','col_1'}, dimensions={0} | all-to-all | bytes 262144 | tf_op jit(solution)/shard_map/all_to_all | solution.py:260
  98.3 1.2 shard_map.127
  99.5 12.4 %all_to_all.64.y = bf16[16,16,128]{2,1,0:T(8,128)(2,1)S(1)} all-to-all(bf16[16,16,128]{2,1,0:T(8,128)(2,1)S(1)} %shard_map.127), channel_id=1, replica_groups=mesh['row_0'=4,'row_1'=2,'core'=2,'col_0'=8,'col_1'=4] {'row_0','row_1',..., dimensions={0} | all-to-all | bytes 131072 | tf_op jit(solution)/shard_map/all_to_all | solution.py:260
  111.9 1.2 shard_map.128
  113.2 12.7 %all_to_all.65.y = bf16[32,16,128]{2,1,0:T(8,128)(2,1)S(1)} all-to-all(bf16[32,16,128]{2,1,0:T(8,128)(2,1)S(1)} %shard_map.128), channel_id=1, replica_groups=mesh['row_0'=4,'row_1'=2,'core'=2,'col_0'=8,'col_1'=4] {'col_0','col_1'}, dimensions={0} | all-to-all | bytes 262144 | tf_op jit(solution)/shard_map/all_to_all | solution.py:260
  125.9 1.2 shard_map.129
  127.1 11.9 %all_to_all.66.y = bf16[16,16,128]{2,1,0:T(8,128)(2,1)S(1)} all-to-all(bf16[16,16,128]{2,1,0:T(8,128)(2,1)S(1)} %shard_map.129), channel_id=1, replica_groups=mesh['row_0'=4,'row_1'=2,'core'=2,'col_0'=8,'col_1'=4] {'row_0','row_1',..., dimensions={0} | all-to-all | bytes 131072 | tf_op jit(solution)/shard_map/all_to_all | solution.py:260
  139.0 1.2 shard_map.130
  140.2 12.8 %all_to_all.67.y = bf16[32,16,128]{2,1,0:T(8,128)(2,1)S(1)} all-to-all(bf16[32,16,128]{2,1,0:T(8,128)(2,1)S(1)} %shard_map.130), channel_id=1, replica_groups=mesh['row_0'=4,'row_1'=2,'core'=2,'col_0'=8,'col_1'=4] {'col_0','col_1'}, dimensions={0} | all-to-all | bytes 262144 | tf_op jit(solution)/shard_map/all_to_all | solution.py:260
  153.0 1.9 shard_map.131
  154.9 4.9 %all-to-all-start.9 = ((bf16[16,16,128]{2,1,0:T(8,128)(2,1)}), bf16[16,16,128]{2,1,0:T(8,128)(2,1)S(1)}, u32[]{:S(2)}, u32[]{:S(2)}) async-start(bf16[16,16,128]{2,1,0:T(8,128)(2,1)} %get-tuple-element.39), calls=%async_computation.9 | async-start | bytes 131072 | tf_op jit(solution)/shard_map/all_to_all | solution.py:260
  159.8 4.1 %shard_map.132 = (f32[16,128]{1,0:T(8,128)}, f32[64,2048]{1,0:T(8,128)S(1)}) custom-call(f32[16,128]{1,0:T(8,128)S(1)} %get-tuple-element.37.row_scale, bf16[64,6144]{1,0:T(8,128)(2,1)S(1)} %reshape.27.src, bf16[2048,2048]{1,0:T(8,128)(2,1)} %copy-done), custom_call_target="tpu_custom_call" | custom-call | tf_op jit(solution)/shard_map/pallas_call | solution.py:249
  163.9 3.7 %all-to-all-done.9.y = bf16[16,16,128]{2,1,0:T(8,128)(2,1)S(1)} async-done(((bf16[16,16,128]{2,1,0:T(8,128)(2,1)}), bf16[16,16,128]{2,1,0:T(8,128)(2,1)S(1)}, u32[]{:S(2)}, u32[]{:S(2)}) %all-to-all-start.9) | async-done | bytes 65568 | tf_op jit(solution)/shard_map/all_to_all | solution.py:260
  168.5 12.2 %all_to_all.68.y = bf16[16,32,128]{2,1,0:T(8,128)(2,1)S(1)} all-to-all(bf16[16,32,128]{2,1,0:T(8,128)(2,1)S(1)} %get-tuple-element.42), channel_id=1, replica_groups=mesh['row_0'=4,'row_1'=2,'core'=2,'col_0'=8,'col_1'=4] {'row_0','row_1',..., dimensions={0} | all-to-all | bytes 262144 | tf_op jit(solution)/shard_map/all_to_all | solution.py:260
  180.8 15.3 %all_to_all.69.y = bf16[32,32,128]{2,1,0:T(8,128)(2,1)S(1)} all-to-all(bf16[32,32,128]{2,1,0:T(8,128)(2,1)S(1)} %shard_map.134), channel_id=1, replica_groups=mesh['row_0'=4,'row_1'=2,'core'=2,'col_0'=8,'col_1'=4] {'col_0','col_1'}, dimensions={0} | all-to-all | bytes 524288 | tf_op jit(solution)/shard_map/all_to_all | solution.py:260
  (10 shorter events, 2.2 us)
Async XLA Ops:
  2.4 35.4 %all-to-all-start = ((bf16[32,2,6144]{2,1,0:T(2,128)(2,1)}), bf16[32,2,6144]{2,1,0:T(2,128)(2,1)S(1)}, u32[]{:S(2)}, u32[]{:S(2)}) async-start(bf16[32,2,6144]{2,1,0:T(2,128)(2,1)} %get-tuple-element.23), calls=%async_computation | async-start | bytes 1572864 | tf_op jit(solution)/shard_map/all_to_all | solution.py:260
  85.8 67.2 %copy-start = (bf16[2048,2048]{1,0:T(8,128)(2,1)}, bf16[2048,2048]{1,0:T(8,128)(2,1)S(1)}, u32[]{:S(2)}) copy-start(bf16[2048,2048]{1,0:T(8,128)(2,1)S(1)} %get-tuple-element.34.kernel) | copy-start | bytes 25165828
  154.9 12.8 %all-to-all-start.9 = ((bf16[16,16,128]{2,1,0:T(8,128)(2,1)}), bf16[16,16,128]{2,1,0:T(8,128)(2,1)S(1)}, u32[]{:S(2)}, u32[]{:S(2)}) async-start(bf16[16,16,128]{2,1,0:T(8,128)(2,1)} %get-tuple-element.39), calls=%async_computation.9 | async-start | bytes 131072 | tf_op jit(solution)/shard_map/all_to_all | solution.py:260
